TPU v7x, 256 devices: a whole 4x4x8 slice. The times are simulated.
256 devices in a mesh: slab: 16 (over z, core), pencil: 16 (over y, x).
Axes of the slice: x: 4, y: 4, z: 8, core: 2. Of those that a mesh axis runs over, the one named last changes fastest.
Arguments:
- fractions: float32 [3, 4194304], P(None, ('slab', 'pencil')), may hold values from 0 to 1
- cell_index: int32 [3, 4194304], P(None, ('slab', 'pencil')), may hold values from 0 to 63, as said below
- weights: bfloat16 [4, 4194304], P(None, ('slab', 'pencil')), may hold values from -6 to 6
- counts: int32 [256, 256, 32], P(('slab', 'pencil')), may hold values from 0 to 2, as said below
- smoothing: float32 [4], replicated, may hold values from 1 to 256
- bias_values: float32 [4], replicated, may hold values from 0.5 to 1.5
- observed: float32 [16, 1024, 1024], P('slab', 'pencil'), may hold values from -6 to 6
- precision: float32 [16, 1024, 1024], P('slab', 'pencil'), may hold values from 0.25 to 4
Outputs:
- particle_grads: float32 [7, 4194304], P(None, ('slab', 'pencil'))
- model_field: bfloat16 [16, 1024, 1024], P('slab', 'pencil')
Inputs may be any that keep to these rules, and one draw needn't show every extreme that they name: counts[s, t, b] is how many of the 2 slots that device s holds for z block b of tile t are live (the first ones); some tile gets 2 for every block from every device. `cell_index`: row 0 is below 1, row 1 below 64, row 2 below 32.
All inputs are finite; a program needn't handle non-finite values.
Results may differ from a plain program's by a relative error of at most 0.0074.
Values may be sent and summed in bfloat16 or wider, within the bound.
No kernel may reach another device: no remote copies, remote signals or barrier semaphores. Data moves between devices by JAX's collectives and lax.ppermute only.
A program may use at most 128 MiB of HBM per device.

v0:
```python
import jax
import jax.numpy as jnp
from jax import lax
from jax.experimental import pallas as pl
from jax.experimental.pallas import tpu as pltpu
from jax.sharding import PartitionSpec as P

NY = 1024
NZ = 1024
ZB = 32
PART_DEV = 16384
TILES = 256
CAP = 2
TY = 64
LANES = 64
RECORD = 12 * LANES
GRADS = 7 * LANES
CH = 4
N_PENCIL = 16
CHUNK = 136
F32 = jnp.float32
BF16 = jnp.bfloat16

R_GX, R_GY, R_GZ, R_LOW, R_CY, R_CZ = 4, 5, 6, 3, 10, 11


def params():
    return pltpu.CompilerParams(vmem_limit_bytes=56 * 1024 * 1024)


def lanes_of(shape):
    return lax.broadcasted_iota(jnp.int32, shape, len(shape) - 1)


def live_table(counts_ref):
    lane = lanes_of((ZB, 128))
    block = lax.broadcasted_iota(jnp.int32, (ZB, 128), 0)
    spread = jnp.where((lane % LANES) // CAP == block, 1.0, 0.0).astype(BF16)
    held = jnp.dot(counts_ref[...].astype(F32).astype(BF16), spread, preferred_element_type=F32)
    rank = (lanes_of((TILES, 128)) % CAP).astype(F32)
    return rank < held


def pack_kernel(fr_ref, ci_ref, wt_ref, cn_ref, out_ref, scr):
    low = lanes_of((128, 128)) < LANES

    def put(j, a, b):
        even = jnp.where(low, a, pltpu.roll(b, LANES, 1))
        odd = jnp.where(low, pltpu.roll(a, LANES, 1), b)
        scr[j, pl.ds(0, 128, stride=2), :] = even
        scr[j, pl.ds(1, 128, stride=2), :] = odd

    put(0, wt_ref[0].astype(F32), wt_ref[1].astype(F32))
    put(1, wt_ref[2].astype(F32), wt_ref[3].astype(F32))
    offsets = [fr_ref[d] - 0.5 for d in range(3)]
    high = [g.astype(BF16).astype(F32) for g in offsets]
    rest = [g - h for g, h in zip(offsets, high)]
    put(2, high[0], high[1])
    put(3, high[2], rest[0])
    put(4, rest[1], rest[2])
    put(5, ci_ref[1].astype(F32), ci_ref[2].astype(F32))
    live = live_table(cn_ref)
    out_ref[:, 0:128] = jnp.where(live, scr[0], 0.0).astype(BF16)
    out_ref[:, 128:256] = jnp.where(live, scr[1], 0.0).astype(BF16)
    for j in range(2, 6):
        out_ref[:, j * 128 : j * 128 + 128] = scr[j].astype(BF16)


def unpack_kernel(in_ref, cn_ref, out_ref, scr):
    live = live_table(cn_ref)
    low = lanes_of((128, 128)) < LANES
    for j in range(4):
        if j < 3:
            scr[...] = jnp.where(live, in_ref[:, j * 128 : j * 128 + 128].astype(F32), 0.0)
        else:
            scr[:, 0:LANES] = jnp.where(live[:, 0:LANES], in_ref[:, 384:GRADS].astype(F32), 0.0)
        even = scr[pl.ds(0, 128, stride=2), :]
        odd = scr[pl.ds(1, 128, stride=2), :]
        out_ref[2 * j] = jnp.where(low, even, pltpu.roll(odd, LANES, 1))
        if j < 3:
            out_ref[2 * j + 1] = jnp.where(low, pltpu.roll(even, LANES, 1), odd)


def transpose_records(x_ref, xt_ref):
    for j in range(6):
        for h in range(2):
            piece = x_ref[h * 128 : h * 128 + 128, j * 128 : j * 128 + 128].astype(F32)
            xt_ref[j * 128 : j * 128 + 128, h * 128 : h * 128 + 128] = piece.T
    first, last = R_GX * LANES, R_GZ * LANES + LANES
    xt_ref[first:last, :] += xt_ref[first + R_LOW * LANES : last + R_LOW * LANES, :]


def slot_row(xt_ref, r, b):
    first = xt_ref[pl.ds(r * LANES + 2 * b, 1), :]
    second = xt_ref[pl.ds(r * LANES + 2 * b + 1, 1), :]
    return jnp.concatenate([first, second], axis=1)


def hat(places, centre):
    return jnp.maximum(1.0 - jnp.abs(places - centre), 0.0)


def rim_places(rows):
    row = lax.broadcasted_iota(jnp.int32, (rows, 128), 0)
    y = jnp.where(row == 64, -1, jnp.where(row == 65, 64, jnp.where(row > 65, 1000, row)))
    return y.astype(F32)


def deposit(xt_ref, acc_ref, yv_ref, zv_ref, side):
    def block(b, carry):
        gx = slot_row(xt_ref, R_GX, b)
        if side == 0:
            wx = 1.0 - jnp.abs(gx)
        elif side < 0:
            wx = jnp.maximum(-gx, 0.0)
        else:
            wx = jnp.maximum(gx, 0.0)
        py = slot_row(xt_ref, R_CY, b) + slot_row(xt_ref, R_GY, b)
        pz = slot_row(xt_ref, R_CZ, b) + slot_row(xt_ref, R_GZ, b) + 8.0
        plane = (wx * hat(yv_ref[...], py)).astype(BF16)
        wz = hat(zv_ref[...], pz)
        column = jnp.concatenate([slot_row(xt_ref, c, b) * wz for c in range(CH)], axis=0).astype(BF16)
        add = lax.dot_general(column, plane, (((1,), (1,)), ((), ())), preferred_element_type=F32)
        at = pl.multiple_of(b * ZB, ZB)
        for c in range(CH):
            acc_ref[c, pl.ds(at, 48), 0:72] += add[c * 48 : c * 48 + 48]
        return carry

    lax.fori_loop(0, NZ // ZB, block, 0, unroll=2)


def fill_places(yv_ref, zv_ref):
    yv = rim_places(72)
    zv = lax.broadcasted_iota(jnp.int32, (48, 128), 0).astype(F32)
    for k in range(4):
        yv_ref[:, k * 128 : k * 128 + 128] = yv
        zv_ref[:, k * 128 : k * 128 + 128] = zv


def own_kernel(x_ref, acc_ref, xt_ref, yv_ref, zv_ref):
    fill_places(yv_ref, zv_ref)
    transpose_records(x_ref, xt_ref)
    acc_ref[...] = jnp.zeros_like(acc_ref)
    deposit(xt_ref, acc_ref, yv_ref, zv_ref, 0)


def along_z(field_ref, col_ref, out_ref):
    def channel(c, carry):
        for half in range(2):
            pair = jnp.concatenate(
                [
                    field_ref[c, (2 * half) * 256 : (2 * half) * 256 + 256, :],
                    field_ref[c, (2 * half + 1) * 256 : (2 * half + 1) * 256 + 256, :],
                ],
                axis=1,
            )
            prods = [
                jnp.dot(col_ref[c, d * 256 : d * 256 + 256, :], pair, preferred_element_type=F32)
                for d in range(4)
            ]
            for j in range(4):
                part = prods[(j - 2 * half) % 4][:, 0:128] + prods[(j - 2 * half - 1) % 4][:, 128:256]
                if half == 0:
                    out_ref[c, j * 256 : j * 256 + 256, :] = part
                else:
                    out_ref[c, j * 256 : j * 256 + 256, :] += part
        return carry

    lax.fori_loop(0, CH, channel, 0)


def rim_rows(parts, rows):
    lane = lanes_of((rows, 128))
    table = jnp.zeros((rows, 128), F32)
    for c in range(CH):
        table = jnp.where(lane // 2 == c, pltpu.roll(parts[c], LANES + 2 * c, 1), table)
    return table.T[0:8]


def forward_kernel(up_ref, dn_ref, start_ref, col_ref, out_ref, acc, xt, yv, zv, dens, smooth):
    fill_places(yv, zv)
    acc[...] = start_ref[...]
    transpose_records(up_ref, xt)
    deposit(xt, acc, yv, zv, 1)
    transpose_records(dn_ref, xt)
    deposit(xt, acc, yv, zv, -1)
    acc[:, 1024:1032, :] += jnp.concatenate(
        [jnp.zeros((CH, 7, 128), F32), acc[:, 7:8, :]], axis=1
    )
    acc[:, 8:16, :] += jnp.concatenate([acc[:, 1032:1033, :], jnp.zeros((CH, 7, 128), F32)], axis=1)
    dens[...] = acc[:, 8:1032, :].astype(BF16)
    along_z(dens, col_ref, smooth)
    low = lanes_of((64, 128)) < LANES

    def send(p, carry):
        at = pl.multiple_of(p * 64, 64)
        parts = [smooth[c, pl.ds(at, 64), :] for c in range(CH)]
        for pair in range(2):
            both = jnp.where(low, parts[2 * pair], pltpu.roll(parts[2 * pair + 1], LANES, 1))
            out_ref[p, pair * 64 : pair * 64 + 64, :] = both.astype(BF16)
        rims = rim_rows(parts, 64)
        out_ref[p, 128:136, :] = jnp.concatenate([rims, jnp.zeros((8, 64), F32)], axis=1).astype(BF16)
        return carry

    lax.fori_loop(0, N_PENCIL, send, 0)


def wrapped_sum(prod):
    blocks = []
    for j in range(4):
        total = prod[0:64, j * 256 : j * 256 + 256]
        for i in range(1, 4):
            d = (j - i) % 4
            total = total + prod[i * 64 : i * 64 + 64, d * 256 : d * 256 + 256]
        blocks.append(total)
    return jnp.concatenate(blocks, axis=1)


def lines_kernel(bias_ref, in_ref, row_ref, rim_ref, obs_ref, prec_ref, model_ref, out_ref, left, back):
    low = lanes_of((64, 128)) < LANES
    for pair in range(2):
        for pp in range(8):
            a = in_ref[2 * pp, pair * 64 : pair * 64 + 64, :].astype(F32)
            b = in_ref[2 * pp + 1, pair * 64 : pair * 64 + 64, :].astype(F32)
            i, at = pp // 2, (pp % 2) * 128
            left[2 * pair, i * 64 : i * 64 + 64, at : at + 128] = jnp.where(
                low, a, pltpu.roll(b, LANES, 1)
            ).astype(BF16)
            left[2 * pair + 1, i * 64 : i * 64 + 64, at : at + 128] = jnp.where(
                low, pltpu.roll(a, LANES, 1), b
            ).astype(BF16)
    which = lax.broadcasted_iota(jnp.int32, (128, 64), 0) % 8 // 2
    bias = jnp.zeros((128, 64), F32)
    for c in range(CH):
        bias = jnp.where(which == c, bias_ref[c], bias)
    rims = jnp.concatenate([in_ref[p, 128:136, 0:64].astype(F32) for p in range(N_PENCIL)], axis=0)
    rims = (rims * bias).T.astype(BF16)
    model = jnp.dot(rims, rim_ref[...], preferred_element_type=F32)
    for c in range(CH):
        prod = jnp.dot(left[c], row_ref[c], preferred_element_type=F32)
        model = model + bias_ref[c] * wrapped_sum(prod)
    model_ref[...] = model.astype(BF16)
    pull = (prec_ref[...] * (model - obs_ref[...])).astype(BF16)
    stacked = jnp.concatenate([pull[:, i * 256 : i * 256 + 256] for i in range(4)], axis=0)
    for c in range(CH):
        prod = jnp.dot(stacked, row_ref[c], preferred_element_type=F32)
        back[c] = bias_ref[c] * wrapped_sum(prod)
    for pair in range(2):
        for pp in range(8):
            a = back[2 * pair, :, pp * 128 : pp * 128 + 128]
            b = back[2 * pair + 1, :, pp * 128 : pp * 128 + 128]
            out_ref[2 * pp, pair * 64 : pair * 64 + 64, :] = jnp.where(
                low, a, pltpu.roll(b, LANES, 1)
            ).astype(BF16)
            out_ref[2 * pp + 1, pair * 64 : pair * 64 + 64, :] = jnp.where(
                low, pltpu.roll(a, LANES, 1), b
            ).astype(BF16)
    rims = lax.dot_general(rim_ref[...], pull, (((1,), (1,)), ((), ())), preferred_element_type=F32)
    rims = jnp.concatenate([rims * bias, jnp.zeros((128, 64), F32)], axis=1).astype(BF16)
    for p in range(N_PENCIL):
        out_ref[p, 128:136, :] = rims[p * 8 : p * 8 + 8]


def adjoint_kernel(in_ref, col_ref, out_ref, field, smooth):
    lane = lanes_of((64, 128))
    low = lane < LANES

    def take(p, carry):
        at = pl.multiple_of(p * 64, 64)
        rims = in_ref[p, 128:136, :].astype(F32)
        table = jnp.concatenate([rims, jnp.zeros((120, 128), F32)], axis=0).T[0:64]
        for pair in range(2):
            both = in_ref[p, pair * 64 : pair * 64 + 64, :].astype(F32)
            for k in range(2):
                c = 2 * pair + k
                main = both if k == 0 else pltpu.roll(both, LANES, 1)
                rim = jnp.where(lane < 66, pltpu.roll(table, LANES - 2 * c, 1), 0.0)
                field[c, pl.ds(at, 64), :] = jnp.where(low, main, rim).astype(BF16)
        return carry

    lax.fori_loop(0, N_PENCIL, take, 0)
    along_z(field, col_ref, smooth)
    wide = lanes_of((128, 128)) < LANES
    for q in range(8):
        parts = [smooth[c, q * 128 : q * 128 + 128, :] for c in range(CH)]
        for pair in range(2):
            both = jnp.where(wide, parts[2 * pair], pltpu.roll(parts[2 * pair + 1], LANES, 1))
            out_ref[pair * 1024 + q * 128 : pair * 1024 + q * 128 + 128, :] = both.astype(BF16)
        out_ref[2048 + q * 8 : 2048 + q * 8 + 8, :] = rim_rows(parts, 128).astype(BF16)


def sample_kernel(xt_ref, own_ref, up_ref, dn_ref, out_ref, field, planes, yv, ot):
    lane = lanes_of((128, 128))
    low = lane < LANES

    def fill(q, carry):
        at = pl.multiple_of(q * 128, 128)
        to = pl.multiple_of(q * 128 + 16, 16)
        rim_at = pl.multiple_of(2048 + q * 8, 8)
        tables = []
        for ref in (own_ref, up_ref, dn_ref):
            rims = ref[pl.ds(rim_at, 8), :].astype(F32)
            tables.append(jnp.concatenate([rims, jnp.zeros((120, 128), F32)], axis=0).T)
        for pair in range(2):
            own = own_ref[pl.ds(pair * 1024 + at, 128), :].astype(F32)
            up = up_ref[pl.ds(pair * 1024 + at, 128), :].astype(F32)
            dn = dn_ref[pl.ds(pair * 1024 + at, 128), :].astype(F32)
            for k in range(2):
                c = 2 * pair + k
                if k == 0:
                    first = jnp.where(low, up, pltpu.roll(dn, LANES, 1))
                    main = own
                else:
                    first = jnp.where(low, pltpu.roll(up, LANES, 1), dn)
                    main = pltpu.roll(own, LANES, 1)
                rim = jnp.zeros((128, 128), F32)
                for s in range(3):
                    here = pltpu.roll(tables[s], LANES + 2 * s - 2 * c, 1)
                    rim = jnp.where((lane - LANES) // 2 == s, here, rim)
                field[c, pl.ds(to, 128), 0:128] = first.astype(BF16)
                field[c, pl.ds(to, 128), 128:256] = jnp.where(low, main, rim).astype(BF16)
        return carry

    lax.fori_loop(0, 8, fill, 0)
    field[:, 0:16, :] = field[:, 1024:1040, :]
    field[:, 1040:1056, :] = field[:, 16:32, :]
    planes[...] = jnp.zeros_like(planes)
    row = lax.broadcasted_iota(jnp.int32, (72, 512), 0)
    yv[...] = jnp.where(row < 64, row, jnp.where(row % 2 == 0, -1, 64)).astype(F32)
    zv = (lax.broadcasted_iota(jnp.int32, (48, 512), 0) + 8).astype(F32)
    part = lax.broadcasted_iota(jnp.int32, (8, 512), 0) // 2

    def block(b, carry):
        gx, gy, gz = (slot_row(xt_ref, r, b) for r in (R_GX, R_GY, R_GZ))
        cy, cz = slot_row(xt_ref, R_CY, b), slot_row(xt_ref, R_CZ, b)
        fall_x, fall_y, fall_z = gx < 0.0, gy < 0.0, gz < 0.0
        wx = [jnp.maximum(-gx, 0.0), jnp.maximum(gx, 0.0), 1.0 - jnp.abs(gx)]
        sx = [jnp.where(fall_x, -1.0, 0.0), jnp.where(fall_x, 0.0, 1.0), jnp.where(fall_x, 1.0, -1.0)]
        places = yv[...]
        wy = hat(places, cy + gy)
        step_y = places - jnp.where(fall_y, cy - 1.0, cy)
        sy = jnp.where(step_y == 0.0, -1.0, jnp.where(step_y == 1.0, 1.0, 0.0))
        for k, (ax, ay) in enumerate(((wx, wy), (sx, wy), (wx, sy))):
            cols = slice(k * 512, k * 512 + 512)
            for s in range(3):
                planes[s * 64 : s * 64 + 64, cols] = (ax[s] * ay[0:64]).astype(BF16)
            rim = jnp.where(
                part == 0, ax[2], jnp.where(part == 1, ax[0], jnp.where(part == 2, ax[1], 0.0))
            )
            rim = rim * ay[64:72]
            planes[192:208, cols] = jnp.concatenate([rim, jnp.zeros((8, 512), F32)], axis=0).astype(BF16)
        at = pl.multiple_of(b * ZB, ZB)
        here = jnp.concatenate([field[c, pl.ds(at, 64), :] for c in range(CH)], axis=0)
        wz = hat(zv, cz + gz + 16.0)
        step_z = zv - jnp.where(fall_z, cz + 15.0, cz + 16.0)
        sz = jnp.where(step_z == 0.0, -1.0, jnp.where(step_z == 1.0, 1.0, 0.0))
        masses = [slot_row(xt_ref, c, b) for c in range(CH)]
        values = jnp.dot(here, planes[:, 0:512], preferred_element_type=F32)
        grads = []
        slope_z = jnp.zeros((1, 512), F32)
        for c in range(CH):
            v = values[c * 64 + 8 : c * 64 + 56]
            grads.append(jnp.sum(v * wz, axis=0, keepdims=True))
            slope_z = slope_z + masses[c] * jnp.sum(v * sz, axis=0, keepdims=True)
        for k in (1, 2):
            slopes = jnp.dot(here, planes[:, k * 512 : k * 512 + 512], preferred_element_type=F32)
            total = jnp.zeros((48, 512), F32)
            for c in range(CH):
                total = total + masses[c] * slopes[c * 64 + 8 : c * 64 + 56]
            grads.append(jnp.sum(total * wz, axis=0, keepdims=True))
        grads.append(slope_z)
        for r in range(7):
            ot[pl.ds(r * LANES + 2 * b, 1), :] = grads[r][:, 0:256]
            ot[pl.ds(r * LANES + 2 * b + 1, 1), :] = grads[r][:, 256:512]
        return carry

    lax.fori_loop(0, NZ // ZB, block, 0, unroll=2)
    for j in range(4):
        wide = 128 if j < 3 else LANES
        for h in range(2):
            piece = ot[j * 128 : j * 128 + wide, h * 128 : h * 128 + 128]
            out_ref[h * 128 : h * 128 + 128, j * 128 : j * 128 + wide] = piece.T.astype(BF16)


def correlation(smoothing, rows, columns):
    distance = jnp.abs(rows - columns)
    distance = jnp.minimum(distance, NY - distance).astype(F32)
    breadth = smoothing
    profile = jnp.exp(-distance * distance / (2.0 * breadth * breadth)) / jnp.sqrt(breadth)
    return (profile + jnp.where(distance == 0.0, 1.0, 0.0)).astype(BF16)


def call(kernel, outs, scratch, cost=None):
    return pl.pallas_call(
        kernel,
        out_shape=outs,
        scratch_shapes=scratch,
        compiler_params=params(),
        cost_estimate=cost,
    )


def shape(dims, kind):
    return jax.ShapeDtypeStruct(dims, kind)


def per_device(fractions, cell_index, weights, counts, smoothing, bias_values, observed, precision):
    both = ("slab", "pencil")
    count = lax.axis_size("slab")
    forth = [(i, (i + 1) % count) for i in range(count)]
    aft = [((i + 1) % count, i) for i in range(count)]

    ids = jnp.arange(NY, dtype=jnp.int32)
    breadth = smoothing[:, None, None]
    k_row = correlation(breadth, ids[None, :256, None], ids[None, None, :])
    k_col = correlation(breadth, ids[None, :, None], ids[None, None, :256])
    rim = jnp.arange(128, dtype=jnp.int32)
    rim_y = (rim // 8 * TY - 1 + rim % 2 * (TY + 1)) % NY
    k_rim = correlation(smoothing[rim % 8 // 2][:, None], rim_y[:, None], ids[None, :])

    table = counts[0]
    records = call(pack_kernel, shape((TILES, RECORD), BF16), [pltpu.VMEM((6, TILES, 128), F32)])(
        fractions.reshape(3, 128, 128),
        cell_index.reshape(3, 128, 128),
        weights.reshape(CH, 128, 128),
        table,
    )
    arrived = lax.all_to_all(records, both, split_axis=0, concat_axis=0, tiled=True)
    from_up = lax.ppermute(arrived, "slab", forth)
    from_dn = lax.ppermute(arrived, "slab", aft)
    places = [pltpu.VMEM((72, 512), F32), pltpu.VMEM((48, 512), F32)]
    acc, turned = call(
        own_kernel, (shape((CH, 1040, 128), F32), shape((RECORD, TILES), F32)), places
    )(arrived)
    lines = call(
        forward_kernel,
        shape((N_PENCIL, CHUNK, 128), BF16),
        [pltpu.VMEM((CH, 1040, 128), F32), pltpu.VMEM((RECORD, TILES), F32)]
        + places
        + [pltpu.VMEM((CH, NZ, 128), BF16), pltpu.VMEM((CH, NZ, 128), F32)],
    )(from_up, from_dn, acc, k_col)
    lines = lax.all_to_all(lines, "pencil", split_axis=0, concat_axis=0, tiled=True)
    model_field, lines = pl.pallas_call(
        lines_kernel,
        out_shape=(shape((64, NY), BF16), shape((N_PENCIL, CHUNK, 128), BF16)),
        in_specs=[pl.BlockSpec(memory_space=pltpu.SMEM)] + [pl.BlockSpec(memory_space=pltpu.VMEM)] * 5,
        scratch_shapes=[pltpu.VMEM((CH, 256, 256), BF16), pltpu.VMEM((CH, 64, NY), F32)],
        compiler_params=params(),
    )(bias_values, lines, k_row, k_rim, observed[0], precision[0])
    lines = lax.all_to_all(lines, "pencil", split_axis=0, concat_axis=0, tiled=True)
    field = call(
        adjoint_kernel,
        shape((2112, 128), BF16),
        [pltpu.VMEM((CH, NZ, 128), BF16), pltpu.VMEM((CH, NZ, 128), F32)],
    )(lines, k_col)
    field_up = lax.ppermute(field, "slab", forth)
    field_dn = lax.ppermute(field, "slab", aft)
    sampled = call(
        sample_kernel,
        shape((TILES, GRADS), BF16),
        [
            pltpu.VMEM((CH, 1056, 256), BF16),
            pltpu.VMEM((256, 1536), BF16),
            pltpu.VMEM((72, 512), F32),
            pltpu.VMEM((GRADS, TILES), F32),
        ],
    )(turned, field, field_up, field_dn)
    came_back = lax.all_to_all(sampled, both, split_axis=0, concat_axis=0, tiled=True)
    grads = call(unpack_kernel, shape((7, 128, 128), F32), [pltpu.VMEM((TILES, 128), F32)])(
        came_back, table
    )
    return (grads.reshape(7, PART_DEV), model_field[None])


def solution(mesh):
    return jax.shard_map(
        per_device,
        mesh=mesh,
        in_specs=(
            P(None, ("slab", "pencil")),
            P(None, ("slab", "pencil")),
            P(None, ("slab", "pencil")),
            P(("slab", "pencil"), None, None),
            P(),
            P(),
            P("slab", "pencil", None),
            P("slab", "pencil", None),
        ),
        out_specs=(P(None, ("slab", "pencil")), P("slab", "pencil", None)),
        check_vma=False,
    )
```

profile of v0, /device:TPU:1, one launch (start us, length us, event | category | flops | bytes accessed | tf_op | source)
XLA Modules:
  0.0 177.6 jit_solution(10278057073008003973)
XLA Ops:
  2.2 1.7 copy.34
  3.8 1.6 copy.35
  7.0 2.2 %shard_map.95 = bf16[256,768]{1,0:T(8,128)(2,1)} custom-call(f32[3,128,128]{2,1,0:T(8,128)} %bitcast.46, s32[3,128,128]{2,1,0:T(8,128)} %bitcast.45, bf16[4,128,128]{2,1,0:T(8,128)(2,1)} %bitcast.48, s32[256,32]{1,0:T(8,128)} %bitcast.41), custom_call_target="tpu_custom_call" | custom-call | tf_op jit(solution)/shard_map/pallas_call | solution.py:422
  9.8 1.9 %reduce = bf16[256,768]{1,0:T(8,128)(2,1)S(1)} reduce(bf16[256,1,768]{2,0,1:T(8,128)(2,1)} %bitcast.40, bf16[]{:T(256)} %broadcast.338), dimensions={1}, to_apply=%copy.15.reduce_sub_computation | reduce | bytes 786434 | tf_op jit(solution)/shard_map/all_to_all | solution.py:428
  12.5 15.7 %all-to-all-start = ((bf16[256,2,384]{2,1,0:T(2,128)(2,1)}), bf16[256,2,384]{2,1,0:T(2,128)(2,1)S(1)}, u32[]{:S(2)}, u32[]{:S(2)}) async-start(bf16[256,2,384]{2,1,0:T(2,128)(2,1)} %reshape.286), calls=%async_computation | async-start | bytes 786432 | tf_op jit(solution)/shard_map/all_to_all | solution.py:428
  29.2 2.2 %fusion.5.col_ref = bf16[4,1024,256]{2,1,0:T(8,128)(2,1)} fusion(f32[1024,256]{1,0:T(8,128)S(1)} %get-tuple-element.15, f32[4]{0:T(128)S(1)} %get-tuple-element.21, f32[4]{0:T(128)S(1)} %get-tuple-element.20, f32[1024,256]{1,0:T(8,128)S(1)} %get-tuple-element.14), kind=kLoop, calls=%fused_computation.7 | loop fusion | flops 4194304 | bytes 4194336 | tf_op jit(solution)/shard_map/convert_element_type | solution.py:390
  31.3 15.3 %all-to-all-done = bf16[256,2,384]{2,1,0:T(2,128)(2,1)S(1)} async-done(((bf16[256,2,384]{2,1,0:T(2,128)(2,1)}), bf16[256,2,384]{2,1,0:T(2,128)(2,1)S(1)}, u32[]{:S(2)}, u32[]{:S(2)}) %all-to-all-start) | async-done | bytes 393248 | tf_op jit(solution)/shard_map/all_to_all | solution.py:428
  47.5 2.2 %fusion.2.row_ref = bf16[4,256,1024]{2,1,0:T(8,128)(2,1)} fusion(f32[256,1024]{1,0:T(8,128)S(1)} %get-tuple-element.13, f32[4]{0:T(128)S(1)} %get-tuple-element.21, f32[4]{0:T(128)S(1)} %get-tuple-element.20, f32[256,1024]{1,0:T(8,128)S(1)} %get-tuple-element.12), kind=kLoop, calls=%fused_computation.3 | loop fusion | flops 4194304 | bytes 4194336 | tf_op jit(solution)/shard_map/convert_element_type | solution.py:390
  49.8 7.3 %shard_map.96 = (f32[4,1040,128]{2,1,0:T(8,128)}, f32[768,256]{1,0:T(8,128)}) custom-call(bf16[256,768]{1,0:T(8,128)(2,1)} %bitcast.39), custom_call_target="tpu_custom_call" | custom-call | tf_op jit(solution)/shard_map/pallas_call | solution.py:432
  58.0 17.2 %shard_map.97 = bf16[16,136,128]{2,1,0:T(8,128)(2,1)} custom-call(bf16[256,768]{1,0:T(8,128)(2,1)} %copy-done.4, bf16[256,768]{1,0:T(8,128)(2,1)} %copy-done.5, f32[4,1040,128]{2,1,0:T(8,128)} %get-tuple-element.7.start_ref, bf16[4,1024,256]{2,1,0:T(8,128)(2,1)} %fusion.5.col_ref), custom_call_target="tpu_custom_call" | custom-call | tf_op jit(solution)/shard_map/pallas_call | solution.py:435
  75.2 3.6 %all-to-all-start.1 = ((bf16[16,136,128]{2,1,0:T(8,128)(2,1)}), bf16[16,136,128]{2,1,0:T(8,128)(2,1)S(1)}, u32[]{:S(2)}, u32[]{:S(2)}) async-start(bf16[16,136,128]{2,1,0:T(8,128)(2,1)} %shard_map.97), calls=%async_computation.1 | async-start | bytes 1114112 | tf_op jit(solution)/shard_map/all_to_all | solution.py:442
  79.5 2.6 %multiply_multiply_fusion = (f32[128]{0:T(128)S(1)}, f32[128]{0:T(128)S(1)}) fusion(f32[]{:T(128)} %bitcast.5, f32[]{:T(128)} %bitcast.4, f32[]{:T(128)} %bitcast.3, f32[]{:T(128)} %bitcast.2), kind=kLoop, calls=%fused_computation.51 | loop fusion | flops 4096 | bytes 1040 | tf_op jit(solution)/shard_map/mul | solution.py:389
  83.2 5.2 %all-to-all-done.1.in_ref = bf16[16,136,128]{2,1,0:T(8,128)(2,1)S(1)} async-done(((bf16[16,136,128]{2,1,0:T(8,128)(2,1)}), bf16[16,136,128]{2,1,0:T(8,128)(2,1)S(1)}, u32[]{:S(2)}, u32[]{:S(2)}) %all-to-all-start.1) | async-done | bytes 557088 | tf_op jit(solution)/shard_map/all_to_all | solution.py:442
  89.2 4.4 %shard_map.98 = (bf16[64,1024]{1,0:T(8,128)(2,1)}, bf16[16,136,128]{2,1,0:T(8,128)(2,1)}) custom-call(f32[4]{0:T(128)} %bias_ref.1, bf16[16,136,128]{2,1,0:T(8,128)(2,1)} %copy-done, bf16[4,256,1024]{2,1,0:T(8,128)(2,1)} %fusion.2.row_ref, bf16[128,1024]{1,0:T(8,128)(2,1)} %fusion.18.rim_ref, f32[64,1024]{1,0:T(8,128)} %bitcast.49, f32[64,1024]{1,0:T(8,128)} %bitcast.50), custom_call_target="tpu_custom_call" | custom-call | tf_op jit(solution)/shard_map/pallas_call | solution.py:443
  93.6 13.5 %all_to_all.32.in_ref = bf16[16,136,128]{2,1,0:T(8,128)(2,1)} all-to-all(bf16[16,136,128]{2,1,0:T(8,128)(2,1)} %get-tuple-element.8), channel_id=1, replica_groups=mesh['slab'=16,'pencil'=16] {'pencil'}, dimensions={0} | all-to-all | bytes 1114112 | tf_op jit(solution)/shard_map/all_to_all | solution.py:450
  107.1 7.9 %shard_map.99.own_ref = bf16[2112,128]{1,0:T(8,128)(2,1)} custom-call(bf16[16,136,128]{2,1,0:T(8,128)(2,1)} %all_to_all.32.in_ref, bf16[4,1024,256]{2,1,0:T(8,128)(2,1)} %fusion.5.col_ref), custom_call_target="tpu_custom_call" | custom-call | tf_op jit(solution)/shard_map/pallas_call | solution.py:451
  115.0 4.9 %collective-permute-start.2 = (bf16[2112,128]{1,0:T(8,128)(2,1)}, bf16[2112,128]{1,0:T(8,128)(2,1)S(1)}, u32[]{:S(2)}, u32[]{:S(2)}) collective-permute-start(bf16[2112,128]{1,0:T(8,128)(2,1)} %shard_map.99.own_ref), channel_id=1, source_target_pairs={{0,16},{16,32},{32,48},{48,64},{64,80},{80,96},{96,112},{112,128},... | collective-permute-start | bytes 1622024 | tf_op jit(solution)/shard_map/ppermute | solution.py:456
  119.9 6.6 %collective-permute-done.2.up_ref = bf16[2112,128]{1,0:T(8,128)(2,1)S(1)} collective-permute-done((bf16[2112,128]{1,0:T(8,128)(2,1)}, bf16[2112,128]{1,0:T(8,128)(2,1)S(1)}, u32[]{:S(2)}, u32[]{:S(2)}) %collective-permute-start.2) | collective-permute-done | bytes 540704 | tf_op jit(solution)/shard_map/ppermute | solution.py:456
  126.6 2.6 %collective-permute-done.3.dn_ref = bf16[2112,128]{1,0:T(8,128)(2,1)S(1)} collective-permute-done((bf16[2112,128]{1,0:T(8,128)(2,1)}, bf16[2112,128]{1,0:T(8,128)(2,1)S(1)}, u32[]{:S(2)}, u32[]{:S(2)}) %collective-permute-start.3) | collective-permute-done | bytes 540704 | tf_op jit(solution)/shard_map/ppermute | solution.py:457
  130.0 18.2 %shard_map.100 = bf16[256,448]{1,0:T(8,128)(2,1)} custom-call(f32[768,256]{1,0:T(8,128)} %get-tuple-element.6.xt_ref, bf16[2112,128]{1,0:T(8,128)(2,1)} %shard_map.99.own_ref, bf16[2112,128]{1,0:T(8,128)(2,1)} %copy-done.2, bf16[2112,128]{1,0:T(8,128)(2,1)} %copy-done.3), custom_call_target="tpu_custom_call" | custom-call | tf_op jit(solution)/shard_map/pallas_call | solution.py:458
  148.2 1.8 reduce.1
  150.1 22.2 %all_to_all.33 = bf16[256,2,224]{2,1,0:T(2,128)(2,1)S(1)} all-to-all(bf16[256,2,224]{2,1,0:T(2,128)(2,1)S(1)} %reshape.288), channel_id=1, replica_groups=mesh['slab'=16,'pencil'=16] {'slab','pencil'}, dimensions={0} | all-to-all | bytes 458752 | tf_op jit(solution)/shard_map/all_to_all | solution.py:468
  173.4 2.1 %shard_map.101 = f32[7,128,128]{2,1,0:T(8,128)} custom-call(bf16[256,448]{1,0:T(8,128)(2,1)} %bitcast.43, s32[256,32]{1,0:T(8,128)} %bitcast.42), custom_call_target="tpu_custom_call" | custom-call | tf_op jit(solution)/shard_map/pallas_call | solution.py:469
  175.6 2.1 %copy.31 = f32[1,7,128,128]{3,1,2,0:T(8,128)} copy(f32[1,7,128,128]{3,2,1,0:T(8,128)} %bitcast.36) | data formatting | bytes 917504
  (37 shorter events, 11.9 us)
Async XLA Ops:
  12.5 34.1 %all-to-all-start = ((bf16[256,2,384]{2,1,0:T(2,128)(2,1)}), bf16[256,2,384]{2,1,0:T(2,128)(2,1)S(1)}, u32[]{:S(2)}, u32[]{:S(2)}) async-start(bf16[256,2,384]{2,1,0:T(2,128)(2,1)} %reshape.286), calls=%async_computation | async-start | bytes 786432 | tf_op jit(solution)/shard_map/all_to_all | solution.py:428
  28.2 1.0 copy-start.6
  47.0 2.7 %copy-start.1 = (bf16[256,1,768]{2,0,1:T(8,128)(2,1)}, bf16[256,1,768]{2,0,1:T(8,128)(2,1)S(1)}, u32[]{:S(2)}) copy-start(bf16[256,1,768]{2,0,1:T(8,128)(2,1)S(1)} %copy.32) | copy-start | bytes 1179652
  47.0 10.1 %collective-permute-start = (bf16[256,768]{1,0:T(8,128)(2,1)S(1)}, bf16[256,768]{1,0:T(8,128)(2,1)S(1)}, u32[]{:S(2)}, u32[]{:S(2)}) collective-permute-start(bf16[256,768]{1,0:T(8,128)(2,1)S(1)} %bitcast.37), channel_id=1, source_target_pairs={{0,16},{16,32},{32,48},{48,64},{64,80},{80,96},{96,112},{112,128},... | collective-permute-start | bytes 1179656 | tf_op jit(solution)/shard_map/ppermute | solution.py:429
  47.0 10.1 %collective-permute-start.1 = (bf16[256,768]{1,0:T(8,128)(2,1)S(1)}, bf16[256,768]{1,0:T(8,128)(2,1)S(1)}, u32[]{:S(2)}, u32[]{:S(2)}) collective-permute-start(bf16[256,768]{1,0:T(8,128)(2,1)S(1)} %bitcast.38), channel_id=1, source_target_pairs={{16,0},{32,16},{48,32},{64,48},{80,64},{96,80},{112,96},{128,112},... | collective-permute-start | bytes 1179656 | tf_op jit(solution)/shard_map/ppermute | solution.py:430
  57.1 0.7 copy-start.4
  57.1 0.9 copy-start.5
  75.2 13.2 %all-to-all-start.1 = ((bf16[16,136,128]{2,1,0:T(8,128)(2,1)}), bf16[16,136,128]{2,1,0:T(8,128)(2,1)S(1)}, u32[]{:S(2)}, u32[]{:S(2)}) async-start(bf16[16,136,128]{2,1,0:T(8,128)(2,1)} %shard_map.97), calls=%async_computation.1 | async-start | bytes 1114112 | tf_op jit(solution)/shard_map/all_to_all | solution.py:442
  88.4 0.8 copy-start
  115.0 11.6 %collective-permute-start.2 = (bf16[2112,128]{1,0:T(8,128)(2,1)}, bf16[2112,128]{1,0:T(8,128)(2,1)S(1)}, u32[]{:S(2)}, u32[]{:S(2)}) collective-permute-start(bf16[2112,128]{1,0:T(8,128)(2,1)} %shard_map.99.own_ref), channel_id=1, source_target_pairs={{0,16},{16,32},{32,48},{48,64},{64,80},{80,96},{96,112},{112,128},... | collective-permute-start | bytes 1622024 | tf_op jit(solution)/shard_map/ppermute | solution.py:456
  119.9 9.3 %collective-permute-start.3 = (bf16[2112,128]{1,0:T(8,128)(2,1)}, bf16[2112,128]{1,0:T(8,128)(2,1)S(1)}, u32[]{:S(2)}, u32[]{:S(2)}) collective-permute-start(bf16[2112,128]{1,0:T(8,128)(2,1)} %shard_map.99.own_ref), channel_id=1, source_target_pairs={{16,0},{32,16},{48,32},{64,48},{80,64},{96,80},{112,96},{128,112},... | collective-permute-start | bytes 1622024 | tf_op jit(solution)/shard_map/ppermute | solution.py:457
  126.5 2.6 %copy-start.2 = (bf16[2112,128]{1,0:T(8,128)(2,1)}, bf16[2112,128]{1,0:T(8,128)(2,1)S(1)}, u32[]{:S(2)}) copy-start(bf16[2112,128]{1,0:T(8,128)(2,1)S(1)} %collective-permute-done.2.up_ref) | copy-start | bytes 1622020
  129.2 0.8 copy-start.3
where the time goes:
time: 178 us
  Pallas kernels  59.3 us (33%)
  blocking collectives  35.7 us (20%)
  waiting for transfers between devices  29.7 us (17%)
  starting transfers between devices  24.7 us (14%)
  local copies, waits for them, and re-layouts  14.7 us (8%)
  other arithmetic  12.7 us (7%)
    all_to_all x1, blocking collectives, per_device(): lax.all_to_all(sampled, both, split_axis=0, concat_axis=0, tiled=True)  22.2 us
    pallas_call x1, Pallas kernels, per_device(): call(sample_kernel, shape((TILES, GRADS), BF16), [pltpu.VMEM((CH, 1056, 2...  18.2 us
    pallas_call x1, Pallas kernels, per_device(): call(forward_kernel, shape((N_PENCIL, CHUNK, 128), BF16), [pltpu.VMEM((CH...  17.2 us
    all_to_all x1, starting transfers between devices, per_device(): lax.all_to_all(records, both, split_axis=0, concat_axis=0, tiled=True)  15.7 us
    all_to_all x1, waiting for transfers between devices, per_device(): lax.all_to_all(records, both, split_axis=0, concat_axis=0, tiled=True)  15.3 us
    all_to_all x1, blocking collectives, per_device(): lax.all_to_all(lines, 'pencil', split_axis=0, concat_axis=0, tiled=True)  13.5 us
    unnamed x24, local copies, waits for them, and re-layouts  12.7 us
    pallas_call x1, Pallas kernels, per_device(): call(adjoint_kernel, shape((2112, 128), BF16), [pltpu.VMEM((CH, NZ, 128),...  7.88 us
  transfers between devices with their start and end apart: 6, of which 4 were waited for; matrix products, arithmetic and copies ran while one was open for 5% of the time, Pallas kernels for 4%

commit v1 on v0

--- a/solution.py
+++ b/solution.py
@@ -24,68 +24,76 @@
 R_GX, R_GY, R_GZ, R_LOW, R_CY, R_CZ = 4, 5, 6, 3, 10, 11
 
 
-def params():
-    return pltpu.CompilerParams(vmem_limit_bytes=56 * 1024 * 1024)
+PAIRS = RECORD // 128
+BACK = 4
+
+
+def params(mebibytes):
+    return pltpu.CompilerParams(vmem_limit_bytes=mebibytes * 1024 * 1024)
 
 
 def lanes_of(shape):
     return lax.broadcasted_iota(jnp.int32, shape, len(shape) - 1)
 
 
-def live_table(counts_ref):
+def live_rows(counts_ref, scr):
     lane = lanes_of((ZB, 128))
     block = lax.broadcasted_iota(jnp.int32, (ZB, 128), 0)
     spread = jnp.where((lane % LANES) // CAP == block, 1.0, 0.0).astype(BF16)
-    held = jnp.dot(counts_ref[...].astype(F32).astype(BF16), spread, preferred_element_type=F32)
+    held = lax.dot_general(
+        counts_ref[...].astype(F32).astype(BF16),
+        spread,
+        (((0,), (0,)), ((), ())),
+        preferred_element_type=F32,
+    )
     rank = (lanes_of((TILES, 128)) % CAP).astype(F32)
-    return rank < held
-
-
-def pack_kernel(fr_ref, ci_ref, wt_ref, cn_ref, out_ref, scr):
+    scr[0:TILES] = jnp.where(rank < held, 1.0, 0.0)
+    return scr[pl.ds(0, 128, stride=2), :] > 0.0, scr[pl.ds(1, 128, stride=2), :] > 0.0
+
+
+def pack_kernel(fr_ref, ci_ref, wt_ref, cn_ref, out_ref, scr, mask):
     low = lanes_of((128, 128)) < LANES
-
-    def put(j, a, b):
+    live = live_rows(cn_ref, mask)
+
+    def put(k, a, b, masked=False):
         even = jnp.where(low, a, pltpu.roll(b, LANES, 1))
         odd = jnp.where(low, pltpu.roll(a, LANES, 1), b)
-        scr[j, pl.ds(0, 128, stride=2), :] = even
-        scr[j, pl.ds(1, 128, stride=2), :] = odd
-
-    put(0, wt_ref[0].astype(F32), wt_ref[1].astype(F32))
-    put(1, wt_ref[2].astype(F32), wt_ref[3].astype(F32))
-    offsets = [fr_ref[d] - 0.5 for d in range(3)]
+        if masked:
+            even, odd = jnp.where(live[0], even, 0.0), jnp.where(live[1], odd, 0.0)
+        scr[pl.ds(k, 128, stride=2 * PAIRS), :] = even
+        scr[pl.ds(PAIRS + k, 128, stride=2 * PAIRS), :] = odd
+
+    weights = wt_ref[...].astype(F32)
+    put(0, weights[:, 0, :], weights[:, 1, :], True)
+    put(1, weights[:, 2, :], weights[:, 3, :], True)
+    offsets = [fr_ref[:, d, :] - 0.5 for d in range(3)]
     high = [g.astype(BF16).astype(F32) for g in offsets]
     rest = [g - h for g, h in zip(offsets, high)]
     put(2, high[0], high[1])
     put(3, high[2], rest[0])
     put(4, rest[1], rest[2])
-    put(5, ci_ref[1].astype(F32), ci_ref[2].astype(F32))
-    live = live_table(cn_ref)
-    out_ref[:, 0:128] = jnp.where(live, scr[0], 0.0).astype(BF16)
-    out_ref[:, 128:256] = jnp.where(live, scr[1], 0.0).astype(BF16)
-    for j in range(2, 6):
-        out_ref[:, j * 128 : j * 128 + 128] = scr[j].astype(BF16)
-
-
-def unpack_kernel(in_ref, cn_ref, out_ref, scr):
-    live = live_table(cn_ref)
+    put(5, ci_ref[:, 1, :].astype(F32), ci_ref[:, 2, :].astype(F32))
+    out_ref[...] = scr[0 : TILES * PAIRS].astype(BF16)
+
+
+def unpack_kernel(in_ref, cn_ref, out_ref, scr, mask):
     low = lanes_of((128, 128)) < LANES
-    for j in range(4):
+    live = live_rows(cn_ref, mask)
+    scr[0 : TILES * BACK] = in_ref[...].astype(F32)
+    for j in range(BACK):
+        even = jnp.where(live[0], scr[pl.ds(j, 128, stride=2 * BACK), :], 0.0)
+        odd = jnp.where(live[1], scr[pl.ds(BACK + j, 128, stride=2 * BACK), :], 0.0)
+        out_ref[:, 2 * j, :] = jnp.where(low, even, pltpu.roll(odd, LANES, 1))
         if j < 3:
-            scr[...] = jnp.where(live, in_ref[:, j * 128 : j * 128 + 128].astype(F32), 0.0)
-        else:
-            scr[:, 0:LANES] = jnp.where(live[:, 0:LANES], in_ref[:, 384:GRADS].astype(F32), 0.0)
-        even = scr[pl.ds(0, 128, stride=2), :]
-        odd = scr[pl.ds(1, 128, stride=2), :]
-        out_ref[2 * j] = jnp.where(low, even, pltpu.roll(odd, LANES, 1))
-        if j < 3:
-            out_ref[2 * j + 1] = jnp.where(low, pltpu.roll(even, LANES, 1), odd)
-
-
-def transpose_records(x_ref, xt_ref):
-    for j in range(6):
+            out_ref[:, 2 * j + 1, :] = jnp.where(low, pltpu.roll(even, LANES, 1), odd)
+
+
+def transpose_records(x_ref, wide, xt_ref):
+    wide[0 : TILES * PAIRS] = x_ref[...].astype(F32)
+    for k in range(PAIRS):
         for h in range(2):
-            piece = x_ref[h * 128 : h * 128 + 128, j * 128 : j * 128 + 128].astype(F32)
-            xt_ref[j * 128 : j * 128 + 128, h * 128 : h * 128 + 128] = piece.T
+            piece = wide[pl.ds(h * 128 * PAIRS + k, 128, stride=PAIRS), :]
+            xt_ref[k * 128 : k * 128 + 128, h * 128 : h * 128 + 128] = piece.T
     first, last = R_GX * LANES, R_GZ * LANES + LANES
     xt_ref[first:last, :] += xt_ref[first + R_LOW * LANES : last + R_LOW * LANES, :]
 
@@ -116,30 +124,30 @@
         else:
             wx = jnp.maximum(gx, 0.0)
         py = slot_row(xt_ref, R_CY, b) + slot_row(xt_ref, R_GY, b)
-        pz = slot_row(xt_ref, R_CZ, b) + slot_row(xt_ref, R_GZ, b) + 8.0
+        pz = slot_row(xt_ref, R_CZ, b) + slot_row(xt_ref, R_GZ, b) + 1.0
         plane = (wx * hat(yv_ref[...], py)).astype(BF16)
         wz = hat(zv_ref[...], pz)
         column = jnp.concatenate([slot_row(xt_ref, c, b) * wz for c in range(CH)], axis=0).astype(BF16)
         add = lax.dot_general(column, plane, (((1,), (1,)), ((), ())), preferred_element_type=F32)
         at = pl.multiple_of(b * ZB, ZB)
         for c in range(CH):
-            acc_ref[c, pl.ds(at, 48), 0:72] += add[c * 48 : c * 48 + 48]
+            acc_ref[c, pl.ds(at, 40), 0:72] += add[c * 40 : c * 40 + 40]
         return carry
 
-    lax.fori_loop(0, NZ // ZB, block, 0, unroll=2)
+    lax.fori_loop(0, NZ // ZB, block, 0, unroll=4)
 
 
 def fill_places(yv_ref, zv_ref):
     yv = rim_places(72)
-    zv = lax.broadcasted_iota(jnp.int32, (48, 128), 0).astype(F32)
+    zv = lax.broadcasted_iota(jnp.int32, (40, 128), 0).astype(F32)
     for k in range(4):
         yv_ref[:, k * 128 : k * 128 + 128] = yv
         zv_ref[:, k * 128 : k * 128 + 128] = zv
 
 
-def own_kernel(x_ref, acc_ref, xt_ref, yv_ref, zv_ref):
+def own_kernel(x_ref, acc_ref, xt_ref, wide, yv_ref, zv_ref):
     fill_places(yv_ref, zv_ref)
-    transpose_records(x_ref, xt_ref)
+    transpose_records(x_ref, wide, xt_ref)
     acc_ref[...] = jnp.zeros_like(acc_ref)
     deposit(xt_ref, acc_ref, yv_ref, zv_ref, 0)
 
@@ -177,18 +185,16 @@
     return table.T[0:8]
 
 
-def forward_kernel(up_ref, dn_ref, start_ref, col_ref, out_ref, acc, xt, yv, zv, dens, smooth):
+def forward_kernel(up_ref, dn_ref, start_ref, col_ref, out_ref, acc, xt, wide, yv, zv, dens, smooth):
     fill_places(yv, zv)
     acc[...] = start_ref[...]
-    transpose_records(up_ref, xt)
+    transpose_records(up_ref, wide, xt)
     deposit(xt, acc, yv, zv, 1)
-    transpose_records(dn_ref, xt)
+    transpose_records(dn_ref, wide, xt)
     deposit(xt, acc, yv, zv, -1)
-    acc[:, 1024:1032, :] += jnp.concatenate(
-        [jnp.zeros((CH, 7, 128), F32), acc[:, 7:8, :]], axis=1
-    )
-    acc[:, 8:16, :] += jnp.concatenate([acc[:, 1032:1033, :], jnp.zeros((CH, 7, 128), F32)], axis=1)
-    dens[...] = acc[:, 8:1032, :].astype(BF16)
+    acc[:, NZ : NZ + 1, :] += acc[:, 0:1, :]
+    acc[:, 1:2, :] += acc[:, NZ + 1 : NZ + 2, :]
+    dens[...] = acc[:, 1 : NZ + 1, :].astype(BF16)
     along_z(dens, col_ref, smooth)
     low = lanes_of((64, 128)) < LANES
 
@@ -289,7 +295,7 @@
         out_ref[2048 + q * 8 : 2048 + q * 8 + 8, :] = rim_rows(parts, 128).astype(BF16)
 
 
-def sample_kernel(xt_ref, own_ref, up_ref, dn_ref, out_ref, field, planes, yv, ot):
+def sample_kernel(xt_ref, own_ref, up_ref, dn_ref, out_ref, field, planes, yv, ot, tall):
     lane = lanes_of((128, 128))
     low = lane < LANES
 
@@ -340,15 +346,19 @@
         wy = hat(places, cy + gy)
         step_y = places - jnp.where(fall_y, cy - 1.0, cy)
         sy = jnp.where(step_y == 0.0, -1.0, jnp.where(step_y == 1.0, 1.0, 0.0))
+        wx16, sx16 = ([a.astype(BF16) for a in ax] for ax in (wx, sx))
+        wy16, sy16 = wy[0:64].astype(BF16), sy[0:64].astype(BF16)
+        for s in range(3):
+            rows = slice(s * 64, s * 64 + 64)
+            planes[rows, 0:512] = (wx[s] * wy[0:64]).astype(BF16)
+            planes[rows, 512:1024] = sx16[s] * wy16
+            planes[rows, 1024:1536] = wx16[s] * sy16
         for k, (ax, ay) in enumerate(((wx, wy), (sx, wy), (wx, sy))):
-            cols = slice(k * 512, k * 512 + 512)
-            for s in range(3):
-                planes[s * 64 : s * 64 + 64, cols] = (ax[s] * ay[0:64]).astype(BF16)
             rim = jnp.where(
                 part == 0, ax[2], jnp.where(part == 1, ax[0], jnp.where(part == 2, ax[1], 0.0))
             )
-            rim = rim * ay[64:72]
-            planes[192:208, cols] = jnp.concatenate([rim, jnp.zeros((8, 512), F32)], axis=0).astype(BF16)
+            rim = jnp.concatenate([rim * ay[64:72], jnp.zeros((8, 512), F32)], axis=0)
+            planes[192:208, k * 512 : k * 512 + 512] = rim.astype(BF16)
         at = pl.multiple_of(b * ZB, ZB)
         here = jnp.concatenate([field[c, pl.ds(at, 64), :] for c in range(CH)], axis=0)
         wz = hat(zv, cz + gz + 16.0)
@@ -375,11 +385,12 @@
         return carry
 
     lax.fori_loop(0, NZ // ZB, block, 0, unroll=2)
-    for j in range(4):
-        wide = 128 if j < 3 else LANES
+    ot[GRADS:, :] = jnp.zeros((LANES, TILES), F32)
+    for j in range(BACK):
         for h in range(2):
-            piece = ot[j * 128 : j * 128 + wide, h * 128 : h * 128 + 128]
-            out_ref[h * 128 : h * 128 + 128, j * 128 : j * 128 + wide] = piece.T.astype(BF16)
+            piece = ot[j * 128 : j * 128 + 128, h * 128 : h * 128 + 128]
+            tall[pl.ds(h * 128 * BACK + j, 128, stride=BACK), :] = piece.T
+    out_ref[...] = tall[0 : TILES * BACK].astype(BF16)
 
 
 def correlation(smoothing, rows, columns):
@@ -390,14 +401,20 @@
     return (profile + jnp.where(distance == 0.0, 1.0, 0.0)).astype(BF16)
 
 
-def call(kernel, outs, scratch, cost=None):
+def call(kernel, outs, scratch, mebibytes):
     return pl.pallas_call(
         kernel,
         out_shape=outs,
         scratch_shapes=scratch,
-        compiler_params=params(),
-        cost_estimate=cost,
+        compiler_params=params(mebibytes),
     )
+
+
+def exchange(rows, wide, axes):
+    rows = rows.reshape(TILES, wide, 2, 128).transpose(0, 2, 1, 3).reshape(TILES, 2, wide * 128)
+    rows = lax.all_to_all(rows, axes, split_axis=0, concat_axis=0, tiled=True)
+    rows = rows.reshape(TILES, 2, wide, 128).transpose(0, 2, 1, 3)
+    return rows.reshape(TILES * 2 * wide, 128)
 
 
 def shape(dims, kind):
@@ -418,26 +435,35 @@
     rim_y = (rim // 8 * TY - 1 + rim % 2 * (TY + 1)) % NY
     k_rim = correlation(smoothing[rim % 8 // 2][:, None], rim_y[:, None], ids[None, :])
 
-    table = counts[0]
-    records = call(pack_kernel, shape((TILES, RECORD), BF16), [pltpu.VMEM((6, TILES, 128), F32)])(
-        fractions.reshape(3, 128, 128),
-        cell_index.reshape(3, 128, 128),
-        weights.reshape(CH, 128, 128),
-        table,
-    )
-    arrived = lax.all_to_all(records, both, split_axis=0, concat_axis=0, tiled=True)
+    table = counts[0].T
+    split = [a.reshape(a.shape[0], 128, 128).transpose(1, 0, 2) for a in (fractions, cell_index, weights)]
+    mask = pltpu.VMEM((TILES + 8, 128), F32)
+    records = call(
+        pack_kernel,
+        shape((TILES * PAIRS, 128), BF16),
+        [pltpu.VMEM((TILES * PAIRS + 16, 128), F32), mask],
+        12,
+    )(*split, table)
+    arrived = exchange(records, PAIRS // 2, both)
+    arrived, k_row, k_col, k_rim = lax.optimization_barrier((arrived, k_row, k_col, k_rim))
     from_up = lax.ppermute(arrived, "slab", forth)
     from_dn = lax.ppermute(arrived, "slab", aft)
-    places = [pltpu.VMEM((72, 512), F32), pltpu.VMEM((48, 512), F32)]
-    acc, turned = call(
-        own_kernel, (shape((CH, 1040, 128), F32), shape((RECORD, TILES), F32)), places
+    turned = pltpu.VMEM((RECORD, TILES), F32)
+    wide = pltpu.VMEM((TILES * PAIRS + 8, 128), F32)
+    places = [pltpu.VMEM((72, 512), F32), pltpu.VMEM((40, 512), F32)]
+    acc, xt = call(
+        own_kernel,
+        (shape((CH, 1040, 128), F32), shape((RECORD, TILES), F32)),
+        [wide] + places,
+        12,
     )(arrived)
     lines = call(
         forward_kernel,
         shape((N_PENCIL, CHUNK, 128), BF16),
-        [pltpu.VMEM((CH, 1040, 128), F32), pltpu.VMEM((RECORD, TILES), F32)]
+        [pltpu.VMEM((CH, 1040, 128), F32), turned, wide]
         + places
         + [pltpu.VMEM((CH, NZ, 128), BF16), pltpu.VMEM((CH, NZ, 128), F32)],
+        24,
     )(from_up, from_dn, acc, k_col)
     lines = lax.all_to_all(lines, "pencil", split_axis=0, concat_axis=0, tiled=True)
     model_field, lines = pl.pallas_call(
@@ -445,31 +471,39 @@
         out_shape=(shape((64, NY), BF16), shape((N_PENCIL, CHUNK, 128), BF16)),
         in_specs=[pl.BlockSpec(memory_space=pltpu.SMEM)] + [pl.BlockSpec(memory_space=pltpu.VMEM)] * 5,
         scratch_shapes=[pltpu.VMEM((CH, 256, 256), BF16), pltpu.VMEM((CH, 64, NY), F32)],
-        compiler_params=params(),
+        compiler_params=params(20),
     )(bias_values, lines, k_row, k_rim, observed[0], precision[0])
     lines = lax.all_to_all(lines, "pencil", split_axis=0, concat_axis=0, tiled=True)
     field = call(
         adjoint_kernel,
         shape((2112, 128), BF16),
         [pltpu.VMEM((CH, NZ, 128), BF16), pltpu.VMEM((CH, NZ, 128), F32)],
+        20,
     )(lines, k_col)
     field_up = lax.ppermute(field, "slab", forth)
     field_dn = lax.ppermute(field, "slab", aft)
     sampled = call(
         sample_kernel,
-        shape((TILES, GRADS), BF16),
+        shape((TILES * BACK, 128), BF16),
         [
             pltpu.VMEM((CH, 1056, 256), BF16),
             pltpu.VMEM((256, 1536), BF16),
             pltpu.VMEM((72, 512), F32),
-            pltpu.VMEM((GRADS, TILES), F32),
+            pltpu.VMEM((BACK * 128, TILES), F32),
+            pltpu.VMEM((TILES * BACK + 8, 128), F32),
         ],
-    )(turned, field, field_up, field_dn)
-    came_back = lax.all_to_all(sampled, both, split_axis=0, concat_axis=0, tiled=True)
-    grads = call(unpack_kernel, shape((7, 128, 128), F32), [pltpu.VMEM((TILES, 128), F32)])(
-        came_back, table
-    )
-    return (grads.reshape(7, PART_DEV), model_field[None])
+        20,
+    )(xt, field, field_up, field_dn)
+    came_back = lax.all_to_all(
+        sampled.reshape(TILES, BACK, 128), both, split_axis=0, concat_axis=0, tiled=True
+    ).reshape(TILES * BACK, 128)
+    grads = call(
+        unpack_kernel,
+        shape((128, 7, 128), F32),
+        [pltpu.VMEM((TILES * BACK + 8, 128), F32), mask],
+        12,
+    )(came_back, table)
+    return (grads.transpose(1, 0, 2).reshape(7, PART_DEV), model_field[None])
 
 
 def solution(mesh):

time: 178 us -> 146 us (0.82)
  Pallas kernels: 59.3 us -> 41.8 us
  blocking collectives: 35.7 us -> 49 us
  waiting for transfers between devices: 29.7 us -> 18.7 us
  local copies, waits for them, and re-layouts: 14.7 us -> 5.04 us
  other arithmetic: 12.7 us -> 7.61 us
  starting transfers between devices: 24.7 us -> 22.6 us
    all_to_all x2 -> x1, waiting for transfers between devices: 20.5 us -> 9.31 us  [exchange(): rows = lax.all_to_all(rows, axes, split_axis=0, concat_axis=0, tiled=True)]
    all_to_all x1 -> x2, blocking collectives: 13.5 us -> 24.6 us  [per_device(): lax.all_to_all(lines, 'pencil', split_axis=0, concat_axis=0, tiled=True)]
    unnamed x24 -> x18, local copies, waits for them, and re-layouts: 12.7 us -> 3.57 us
    ppermute x1, waiting for transfers between devices: 6.61 us -> 0.01 us  [per_device(): field_up = lax.ppermute(field, 'slab', forth)]
    pallas_call x1, Pallas kernels: 17.2 us -> 11.6 us  [per_device(): call(forward_kernel, shape((N_PENCIL, CHUNK, 128), BF16), [pltpu.VMEM((CH...]
    ppermute x1, waiting for transfers between devices: 2.64 us -> 7.32 us  [per_device(): field_dn = lax.ppermute(field, 'slab', aft)]
    ppermute x1, starting transfers between devices: 0.01 us -> 4.48 us  [per_device(): field_dn = lax.ppermute(field, 'slab', aft)]
    ppermute x1, starting transfers between devices: 4.94 us -> 0.74 us  [per_device(): field_up = lax.ppermute(field, 'slab', forth)]
  transfers between devices with their start and end apart: 6 -> 5, of which waited for: 4 -> 3; matrix products, arithmetic and copies ran while one was open for 5% -> 6% of each run, Pallas kernels for 4% -> 3%
where the time goes in v1:
time: 146 us
  blocking collectives  49 us (34%)
  Pallas kernels  41.8 us (29%)
  starting transfers between devices  22.6 us (15%)
  waiting for transfers between devices  18.7 us (13%)
  other arithmetic  7.61 us (5%)
  local copies, waits for them, and re-layouts  5.04 us (3%)
    all_to_all x2, blocking collectives, per_device(): lax.all_to_all(lines, 'pencil', split_axis=0, concat_axis=0, tiled=True)  24.6 us
    all_to_all x1, blocking collectives, per_device(): lax.all_to_all(sampled.reshape(TILES, BACK, 128), both, split_axis=0, con...  24.3 us
    pallas_call x1, Pallas kernels, per_device(): call(sample_kernel, shape((TILES * BACK, 128), BF16), [pltpu.VMEM((CH, 10...  16 us
    all_to_all x1, starting transfers between devices, exchange(): rows = lax.all_to_all(rows, axes, split_axis=0, concat_axis=0, tiled=True)  15.7 us
    pallas_call x1, Pallas kernels, per_device(): call(forward_kernel, shape((N_PENCIL, CHUNK, 128), BF16), [pltpu.VMEM((CH...  11.6 us
    all_to_all x1, waiting for transfers between devices, exchange(): rows = lax.all_to_all(rows, axes, split_axis=0, concat_axis=0, tiled=True)  9.31 us
    ppermute x1, waiting for transfers between devices, per_device(): field_dn = lax.ppermute(field, 'slab', aft)  7.32 us
    pallas_call x1, Pallas kernels, per_device(): call(adjoint_kernel, shape((2112, 128), BF16), [pltpu.VMEM((CH, NZ, 128),...  5.29 us
  transfers between devices with their start and end apart: 5, of which 3 were waited for; matrix products, arithmetic and copies ran while one was open for 6% of the time, Pallas kernels for 3%

profile of v1, /device:TPU:1, one launch (start us, length us, event | category | flops | bytes accessed | tf_op | source)
XLA Modules:
  0.0 145.5 jit_solution(322430030494826650)
XLA Ops:
  0.6 0.9 copy-done.3
  1.6 0.9 copy-done.4
  2.5 0.9 copy-done.5
  3.4 0.8 copy-done.6
  4.2 1.7 %shard_map.95 = bf16[1536,128]{1,0:T(8,128)(2,1)} custom-call(f32[128,3,128]{2,1,0:T(4,128)S(1)} %bitcast.44, s32[128,3,128]{2,1,0:T(4,128)S(1)} %bitcast.45, bf16[128,4,128]{2,1,0:T(4,128)(2,1)S(1)} %bitcast.46, s32[32,256]{1,0:T(8,128)S(1)} %bitcast.47), custom_call_target="tpu_custom_call" | custom-call | tf_op jit(solution)/shard_map/pallas_call | solution.py:441
  5.9 15.7 %all-to-all-start = ((bf16[256,2,384]{2,1,0:T(2,128)(2,1)}), bf16[256,2,384]{2,1,0:T(2,128)(2,1)S(1)}, u32[]{:S(2)}, u32[]{:S(2)}) async-start(bf16[256,2,384]{2,1,0:T(2,128)(2,1)} %bitcast.10), calls=%async_computation | async-start | bytes 786432 | tf_op jit(solution)/shard_map/all_to_all | solution.py:415
  22.2 1.5 fusion.26
  24.6 2.5 %multiply_multiply_fusion = (f32[128]{0:T(128)S(1)}, f32[128]{0:T(128)S(1)}) fusion(f32[]{:T(128)} %bitcast.17, f32[]{:T(128)} %bitcast.16, f32[]{:T(128)} %bitcast.15, f32[]{:T(128)} %bitcast.14), kind=kLoop, calls=%fused_computation.45 | loop fusion | flops 4096 | bytes 1040 | tf_op jit(solution)/shard_map/mul | solution.py:400
  27.6 2.2 %fusion.5.row_ref = bf16[4,256,1024]{2,1,0:T(8,128)(2,1)} fusion(f32[256,1024]{1,0:T(8,128)S(1)} %get-tuple-element.23, f32[4]{0:T(128)S(1)} %get-tuple-element.29, f32[4]{0:T(128)S(1)} %get-tuple-element.28, f32[256,1024]{1,0:T(8,128)S(1)} %get-tuple-element.22), kind=kLoop, calls=%fused_computation.7 | loop fusion | flops 4194304 | bytes 4194336 | tf_op jit(solution)/shard_map/convert_element_type | solution.py:401
  29.8 0.9 fusion.2.col_ref
  30.7 9.3 %all-to-all-done = bf16[256,2,384]{2,1,0:T(2,128)(2,1)S(1)} async-done(((bf16[256,2,384]{2,1,0:T(2,128)(2,1)}), bf16[256,2,384]{2,1,0:T(2,128)(2,1)S(1)}, u32[]{:S(2)}, u32[]{:S(2)}) %all-to-all-start) | async-done | bytes 393248 | tf_op jit(solution)/shard_map/all_to_all | solution.py:415
  40.0 1.7 %collective-permute-start = (bf16[1536,128]{1,0:T(8,128)(2,1)S(1)}, bf16[1536,128]{1,0:T(8,128)(2,1)S(1)}, u32[]{:S(2)}, u32[]{:S(2)}) collective-permute-start(bf16[1536,128]{1,0:T(8,128)(2,1)S(1)} %bitcast.38), channel_id=1, source_target_pairs={{0,16},{16,32},{32,48},{48,64},{64,80},{80,96},{96,112},{112,128},... | collective-permute-start | bytes 1179656 | tf_op jit(solution)/shard_map/ppermute | solution.py:449
  41.7 3.7 %shard_map.96 = (f32[4,1040,128]{2,1,0:T(8,128)S(1)}, f32[768,256]{1,0:T(8,128)S(1)}) custom-call(bf16[1536,128]{1,0:T(8,128)(2,1)S(1)} %bitcast.39), custom_call_target="tpu_custom_call" | custom-call | tf_op jit(solution)/shard_map/pallas_call | solution.py:454
  45.4 2.1 %collective-permute-done.1.dn_ref = bf16[1536,128]{1,0:T(8,128)(2,1)S(1)} collective-permute-done((bf16[1536,128]{1,0:T(8,128)(2,1)S(1)}, bf16[1536,128]{1,0:T(8,128)(2,1)S(1)}, u32[]{:S(2)}, u32[]{:S(2)}) %collective-permute-start.1) | collective-permute-done | bytes 393248 | tf_op jit(solution)/shard_map/ppermute | solution.py:450
  47.5 11.6 %shard_map.97 = bf16[16,136,128]{2,1,0:T(8,128)(2,1)S(1)} custom-call(bf16[1536,128]{1,0:T(8,128)(2,1)S(1)} %collective-permute-done.up_ref, bf16[1536,128]{1,0:T(8,128)(2,1)S(1)} %collective-permute-done.1.dn_ref, f32[4,1040,128]{2,1,0:T(8,128)S(1)} %get-tuple-element.12.start_ref, bf16[4,1024,256]{2,1,0:T(8,128)(2,1)S(1)} %fusion.2.col_ref), custom_call_target="tpu_custom_call" | custom-call | tf_op jit(solution)/shard_map/pallas_call | solution.py:460
  59.1 12.7 %all_to_all.20.in_ref = bf16[16,136,128]{2,1,0:T(8,128)(2,1)S(1)} all-to-all(bf16[16,136,128]{2,1,0:T(8,128)(2,1)S(1)} %shard_map.97), channel_id=1, replica_groups=mesh['slab'=16,'pencil'=16] {'pencil'}, dimensions={0} | all-to-all | bytes 1114112 | tf_op jit(solution)/shard_map/all_to_all | solution.py:468
  71.8 2.2 %shard_map.98 = (bf16[64,1024]{1,0:T(8,128)(2,1)}, bf16[16,136,128]{2,1,0:T(8,128)(2,1)S(1)}) custom-call(f32[4]{0:T(128)S(1)} %copy-done.8, bf16[16,136,128]{2,1,0:T(8,128)(2,1)S(1)} %all_to_all.20.in_ref, bf16[4,256,1024]{2,1,0:T(8,128)(2,1)S(1)} %copy-done, bf16[128,1024]{1,0:T(8,128)(2,1)S(1)} %fusion.18.rim_ref, f32[64,1024]{1,0:T(8,128)S(1)} %bitcast.42, ...), custom_call_target="tpu_custom_call" | custom-call | tf_op jit(solution)/shard_map/pallas_call | solution.py:469
  74.0 11.9 %all_to_all.21.in_ref = bf16[16,136,128]{2,1,0:T(8,128)(2,1)S(1)} all-to-all(bf16[16,136,128]{2,1,0:T(8,128)(2,1)S(1)} %get-tuple-element.16), channel_id=1, replica_groups=mesh['slab'=16,'pencil'=16] {'pencil'}, dimensions={0} | all-to-all | bytes 1114112 | tf_op jit(solution)/shard_map/all_to_all | solution.py:476
  86.0 5.3 %shard_map.99.own_ref = bf16[2112,128]{1,0:T(8,128)(2,1)S(1)} custom-call(bf16[16,136,128]{2,1,0:T(8,128)(2,1)S(1)} %all_to_all.21.in_ref, bf16[4,1024,256]{2,1,0:T(8,128)(2,1)S(1)} %fusion.2.col_ref), custom_call_target="tpu_custom_call" | custom-call | tf_op jit(solution)/shard_map/pallas_call | solution.py:477
  91.3 4.5 %collective-permute-start.3 = (bf16[2112,128]{1,0:T(8,128)(2,1)S(1)}, bf16[2112,128]{1,0:T(8,128)(2,1)S(1)}, u32[]{:S(2)}, u32[]{:S(2)}) collective-permute-start(bf16[2112,128]{1,0:T(8,128)(2,1)S(1)} %shard_map.99.own_ref), channel_id=1, source_target_pairs={{16,0},{32,16},{48,32},{64,48},{80,64},{96,80},{112,96},{128,112},... | collective-permute-start | bytes 1622024 | tf_op jit(solution)/shard_map/ppermute | solution.py:484
  96.5 7.3 %collective-permute-done.3.dn_ref = bf16[2112,128]{1,0:T(8,128)(2,1)S(1)} collective-permute-done((bf16[2112,128]{1,0:T(8,128)(2,1)S(1)}, bf16[2112,128]{1,0:T(8,128)(2,1)S(1)}, u32[]{:S(2)}, u32[]{:S(2)}) %collective-permute-start.3) | collective-permute-done | bytes 540704 | tf_op jit(solution)/shard_map/ppermute | solution.py:484
  103.8 16.0 %shard_map.100 = bf16[1024,128]{1,0:T(8,128)(2,1)S(1)} custom-call(f32[768,256]{1,0:T(8,128)S(1)} %get-tuple-element.11.xt_ref, bf16[2112,128]{1,0:T(8,128)(2,1)S(1)} %shard_map.99.own_ref, bf16[2112,128]{1,0:T(8,128)(2,1)S(1)} %collective-permute-done.2.up_ref, bf16[2112,128]{1,0:T(8,128)(2,1)S(1)} %collective-permute-done.3.dn_ref), custom_call_target="tpu_custom_call" | custom-call | tf_op jit(solution)/shard_map/pallas_call | solution.py:485
  119.8 24.3 %all_to_all.22 = bf16[256,4,128]{2,1,0:T(4,128)(2,1)S(1)} all-to-all(bf16[256,4,128]{2,1,0:T(4,128)(2,1)S(1)} %bitcast.41), channel_id=1, replica_groups=mesh['slab'=16,'pencil'=16] {'slab','pencil'}, dimensions={0} | all-to-all | bytes 524288 | tf_op jit(solution)/shard_map/all_to_all | solution.py:497
  144.2 1.3 shard_map.101
  (26 shorter events, 2.8 us)
Async XLA Ops:
  0.6 1.0 copy-start.3
  1.6 0.9 copy-start.4
  2.5 0.9 copy-start.5
  3.4 0.8 copy-start.6
  5.9 34.1 %all-to-all-start = ((bf16[256,2,384]{2,1,0:T(2,128)(2,1)}), bf16[256,2,384]{2,1,0:T(2,128)(2,1)S(1)}, u32[]{:S(2)}, u32[]{:S(2)}) async-start(bf16[256,2,384]{2,1,0:T(2,128)(2,1)} %bitcast.10), calls=%async_computation | async-start | bytes 786432 | tf_op jit(solution)/shard_map/all_to_all | solution.py:415
  40.0 7.5 %collective-permute-start.1 = (bf16[1536,128]{1,0:T(8,128)(2,1)S(1)}, bf16[1536,128]{1,0:T(8,128)(2,1)S(1)}, u32[]{:S(2)}, u32[]{:S(2)}) collective-permute-start(bf16[1536,128]{1,0:T(8,128)(2,1)S(1)} %bitcast.37), channel_id=1, source_target_pairs={{16,0},{32,16},{48,32},{64,48},{80,64},{96,80},{112,96},{128,112},... | collective-permute-start | bytes 1179656 | tf_op jit(solution)/shard_map/ppermute | solution.py:450
  40.0 7.5 %collective-permute-start = (bf16[1536,128]{1,0:T(8,128)(2,1)S(1)}, bf16[1536,128]{1,0:T(8,128)(2,1)S(1)}, u32[]{:S(2)}, u32[]{:S(2)}) collective-permute-start(bf16[1536,128]{1,0:T(8,128)(2,1)S(1)} %bitcast.38), channel_id=1, source_target_pairs={{0,16},{16,32},{32,48},{48,64},{64,80},{80,96},{96,112},{112,128},... | collective-permute-start | bytes 1179656 | tf_op jit(solution)/shard_map/ppermute | solution.py:449
  47.5 24.3 %copy-start = (bf16[4,256,1024]{2,1,0:T(8,128)(2,1)S(1)}, bf16[4,256,1024]{2,1,0:T(8,128)(2,1)}, u32[]{:S(2)}) copy-start(bf16[4,256,1024]{2,1,0:T(8,128)(2,1)} %fusion.5.row_ref) | copy-start | bytes 6291460
  47.5 24.3 %copy-start.1 = (f32[1,64,1024]{2,1,0:T(8,128)S(1)}, f32[1,64,1024]{2,1,0:T(8,128)}, u32[]{:S(2)}) copy-start(f32[1,64,1024]{2,1,0:T(8,128)} %param.14) | copy-start | bytes 786436
  47.5 24.3 %copy-start.2 = (f32[1,64,1024]{2,1,0:T(8,128)S(1)}, f32[1,64,1024]{2,1,0:T(8,128)}, u32[]{:S(2)}) copy-start(f32[1,64,1024]{2,1,0:T(8,128)} %param.15) | copy-start | bytes 786436
  47.5 24.3 %copy-start.8 = (f32[4]{0:T(128)S(1)}, f32[4]{0:T(128)}, u32[]{:S(2)}) copy-start(f32[4]{0:T(128)} %bias_ref.1) | copy-start | bytes 52
  91.3 52.9 %copy-start.7 = (s32[1,256,32]{1,2,0:T(8,128)S(1)}, s32[1,256,32]{1,2,0:T(8,128)}, u32[]{:S(2)}) copy-start(s32[1,256,32]{1,2,0:T(8,128)} %param.11) | copy-start | bytes 98308
  91.3 12.5 %collective-permute-start.3 = (bf16[2112,128]{1,0:T(8,128)(2,1)S(1)}, bf16[2112,128]{1,0:T(8,128)(2,1)S(1)}, u32[]{:S(2)}, u32[]{:S(2)}) collective-permute-start(bf16[2112,128]{1,0:T(8,128)(2,1)S(1)} %shard_map.99.own_ref), channel_id=1, source_target_pairs={{16,0},{32,16},{48,32},{64,48},{80,64},{96,80},{112,96},{128,112},... | collective-permute-start | bytes 1622024 | tf_op jit(solution)/shard_map/ppermute | solution.py:484
  95.8 8.1 %collective-permute-start.2 = (bf16[2112,128]{1,0:T(8,128)(2,1)S(1)}, bf16[2112,128]{1,0:T(8,128)(2,1)S(1)}, u32[]{:S(2)}, u32[]{:S(2)}) collective-permute-start(bf16[2112,128]{1,0:T(8,128)(2,1)S(1)} %shard_map.99.own_ref), channel_id=1, source_target_pairs={{0,16},{16,32},{32,48},{48,64},{64,80},{80,96},{96,112},{112,128},... | collective-permute-start | bytes 1622024 | tf_op jit(solution)/shard_map/ppermute | solution.py:483

commit v2 on v1

--- a/solution.py
+++ b/solution.py
@@ -1,3 +1,5 @@
+import functools
+
 import jax
 import jax.numpy as jnp
 from jax import lax
@@ -134,7 +136,7 @@
             acc_ref[c, pl.ds(at, 40), 0:72] += add[c * 40 : c * 40 + 40]
         return carry
 
-    lax.fori_loop(0, NZ // ZB, block, 0, unroll=4)
+    lax.fori_loop(0, NZ // ZB, block, 0, unroll=16)
 
 
 def fill_places(yv_ref, zv_ref):
@@ -152,36 +154,32 @@
     deposit(xt_ref, acc_ref, yv_ref, zv_ref, 0)
 
 
-def along_z(field_ref, col_ref, out_ref):
+def along_z(field_ref, col_ref, out_ref, first, count):
     def channel(c, carry):
-        for half in range(2):
-            pair = jnp.concatenate(
-                [
-                    field_ref[c, (2 * half) * 256 : (2 * half) * 256 + 256, :],
-                    field_ref[c, (2 * half + 1) * 256 : (2 * half + 1) * 256 + 256, :],
-                ],
-                axis=1,
+        quarters = [field_ref[c, i * 256 : i * 256 + 256, :] for i in range(4)]
+        pairs = [jnp.concatenate(quarters[i : i + 2], axis=1) for i in (0, 2)]
+        right = jnp.concatenate(pairs, axis=0)
+        cols = [col_ref[first + c, d * 256 : d * 256 + 256, :] for d in range(4)]
+        prods = [
+            jnp.dot(
+                jnp.concatenate([cols[d], cols[(d - 2) % 4]], axis=1),
+                right,
+                preferred_element_type=F32,
             )
-            prods = [
-                jnp.dot(col_ref[c, d * 256 : d * 256 + 256, :], pair, preferred_element_type=F32)
-                for d in range(4)
-            ]
-            for j in range(4):
-                part = prods[(j - 2 * half) % 4][:, 0:128] + prods[(j - 2 * half - 1) % 4][:, 128:256]
-                if half == 0:
-                    out_ref[c, j * 256 : j * 256 + 256, :] = part
-                else:
-                    out_ref[c, j * 256 : j * 256 + 256, :] += part
+            for d in range(4)
+        ]
+        for j in range(4):
+            out_ref[c, j * 256 : j * 256 + 256, :] = prods[j][:, 0:128] + prods[(j - 1) % 4][:, 128:256]
         return carry
 
-    lax.fori_loop(0, CH, channel, 0)
+    lax.fori_loop(0, count, channel, 0, unroll=2)
 
 
 def rim_rows(parts, rows):
     lane = lanes_of((rows, 128))
     table = jnp.zeros((rows, 128), F32)
-    for c in range(CH):
-        table = jnp.where(lane // 2 == c, pltpu.roll(parts[c], LANES + 2 * c, 1), table)
+    for c, part in enumerate(parts):
+        table = jnp.where(lane // 2 == c, pltpu.roll(part, LANES + 2 * c, 1), table)
     return table.T[0:8]
 
 
@@ -195,7 +193,7 @@
     acc[:, NZ : NZ + 1, :] += acc[:, 0:1, :]
     acc[:, 1:2, :] += acc[:, NZ + 1 : NZ + 2, :]
     dens[...] = acc[:, 1 : NZ + 1, :].astype(BF16)
-    along_z(dens, col_ref, smooth)
+    along_z(dens, col_ref, smooth, 0, CH)
     low = lanes_of((64, 128)) < LANES
 
     def send(p, carry):
@@ -208,7 +206,7 @@
         out_ref[p, 128:136, :] = jnp.concatenate([rims, jnp.zeros((8, 64), F32)], axis=1).astype(BF16)
         return carry
 
-    lax.fori_loop(0, N_PENCIL, send, 0)
+    lax.fori_loop(0, N_PENCIL, send, 0, unroll=16)
 
 
 def wrapped_sum(prod):
@@ -267,7 +265,7 @@
         out_ref[p, 128:136, :] = rims[p * 8 : p * 8 + 8]
 
 
-def adjoint_kernel(in_ref, col_ref, out_ref, field, smooth):
+def adjoint_kernel(pair, in_ref, col_ref, out_ref, field, smooth):
     lane = lanes_of((64, 128))
     low = lane < LANES
 
@@ -275,42 +273,60 @@
         at = pl.multiple_of(p * 64, 64)
         rims = in_ref[p, 128:136, :].astype(F32)
         table = jnp.concatenate([rims, jnp.zeros((120, 128), F32)], axis=0).T[0:64]
-        for pair in range(2):
-            both = in_ref[p, pair * 64 : pair * 64 + 64, :].astype(F32)
-            for k in range(2):
-                c = 2 * pair + k
-                main = both if k == 0 else pltpu.roll(both, LANES, 1)
-                rim = jnp.where(lane < 66, pltpu.roll(table, LANES - 2 * c, 1), 0.0)
-                field[c, pl.ds(at, 64), :] = jnp.where(low, main, rim).astype(BF16)
+        both = in_ref[p, pair * 64 : pair * 64 + 64, :].astype(F32)
+        for k in range(2):
+            main = both if k == 0 else pltpu.roll(both, LANES, 1)
+            rim = jnp.where(lane < 66, pltpu.roll(table, LANES - 2 * (2 * pair + k), 1), 0.0)
+            field[k, pl.ds(at, 64), :] = jnp.where(low, main, rim).astype(BF16)
         return carry
 
-    lax.fori_loop(0, N_PENCIL, take, 0)
-    along_z(field, col_ref, smooth)
+    lax.fori_loop(0, N_PENCIL, take, 0, unroll=4)
+    along_z(field, col_ref, smooth, 2 * pair, 2)
     wide = lanes_of((128, 128)) < LANES
     for q in range(8):
-        parts = [smooth[c, q * 128 : q * 128 + 128, :] for c in range(CH)]
-        for pair in range(2):
-            both = jnp.where(wide, parts[2 * pair], pltpu.roll(parts[2 * pair + 1], LANES, 1))
-            out_ref[pair * 1024 + q * 128 : pair * 1024 + q * 128 + 128, :] = both.astype(BF16)
-        out_ref[2048 + q * 8 : 2048 + q * 8 + 8, :] = rim_rows(parts, 128).astype(BF16)
-
-
-def sample_kernel(xt_ref, own_ref, up_ref, dn_ref, out_ref, field, planes, yv, ot, tall):
+        parts = [smooth[k, q * 128 : q * 128 + 128, :] for k in range(2)]
+        both = jnp.where(wide, parts[0], pltpu.roll(parts[1], LANES, 1))
+        out_ref[q * 128 : q * 128 + 128, :] = both.astype(BF16)
+        out_ref[NZ + q * 8 : NZ + q * 8 + 8, :] = rim_rows(parts, 128).astype(BF16)
+
+
+def write_planes(xt_ref, b, places, planes):
+    gx, gy, cy = (slot_row(xt_ref, r, b) for r in (R_GX, R_GY, R_CY))
+    fall_x, fall_y = gx < 0.0, gy < 0.0
+    wx = [jnp.maximum(-gx, 0.0), jnp.maximum(gx, 0.0), 1.0 - jnp.abs(gx)]
+    sx = [jnp.where(fall_x, -1.0, 0.0), jnp.where(fall_x, 0.0, 1.0), jnp.where(fall_x, 1.0, -1.0)]
+    wy = hat(places, cy + gy)
+    step_y = places - jnp.where(fall_y, cy - 1.0, cy)
+    sy = jnp.where(step_y == 0.0, -1.0, jnp.where(step_y == 1.0, 1.0, 0.0))
+    wx16, sx16 = ([a.astype(BF16) for a in ax] for ax in (wx, sx))
+    wy16, sy16 = wy[0:64].astype(BF16), sy[0:64].astype(BF16)
+    for s in range(3):
+        rows = slice(s * 64, s * 64 + 64)
+        planes[rows, 0:512] = (wx[s] * wy[0:64]).astype(BF16)
+        planes[rows, 512:1024] = sx16[s] * wy16
+        planes[rows, 1024:1536] = wx16[s] * sy16
+    part = lax.broadcasted_iota(jnp.int32, (8, 512), 0) // 2
+    for k, (ax, ay) in enumerate(((wx, wy), (sx, wy), (wx, sy))):
+        rim = jnp.where(
+            part == 0, ax[2], jnp.where(part == 1, ax[0], jnp.where(part == 2, ax[1], 0.0))
+        )
+        rim = jnp.concatenate([rim * ay[64:72], jnp.zeros((8, 512), F32)], axis=0)
+        planes[192:208, k * 512 : k * 512 + 512] = rim.astype(BF16)
+
+
+def fill_field(refs, field):
     lane = lanes_of((128, 128))
     low = lane < LANES
 
     def fill(q, carry):
         at = pl.multiple_of(q * 128, 128)
-        to = pl.multiple_of(q * 128 + 16, 16)
-        rim_at = pl.multiple_of(2048 + q * 8, 8)
-        tables = []
-        for ref in (own_ref, up_ref, dn_ref):
-            rims = ref[pl.ds(rim_at, 8), :].astype(F32)
-            tables.append(jnp.concatenate([rims, jnp.zeros((120, 128), F32)], axis=0).T)
+        rim_at = pl.multiple_of(NZ + q * 8, 8)
         for pair in range(2):
-            own = own_ref[pl.ds(pair * 1024 + at, 128), :].astype(F32)
-            up = up_ref[pl.ds(pair * 1024 + at, 128), :].astype(F32)
-            dn = dn_ref[pl.ds(pair * 1024 + at, 128), :].astype(F32)
+            tables = []
+            for ref in refs[pair]:
+                rims = ref[pl.ds(rim_at, 8), :].astype(F32)
+                tables.append(jnp.concatenate([rims, jnp.zeros((120, 128), F32)], axis=0).T)
+            own, up, dn = (ref[pl.ds(at, 128), :].astype(F32) for ref in refs[pair])
             for k in range(2):
                 c = 2 * pair + k
                 if k == 0:
@@ -321,71 +337,59 @@
                     main = pltpu.roll(own, LANES, 1)
                 rim = jnp.zeros((128, 128), F32)
                 for s in range(3):
-                    here = pltpu.roll(tables[s], LANES + 2 * s - 2 * c, 1)
+                    here = pltpu.roll(tables[s], LANES + 2 * s - 2 * k, 1)
                     rim = jnp.where((lane - LANES) // 2 == s, here, rim)
-                field[c, pl.ds(to, 128), 0:128] = first.astype(BF16)
-                field[c, pl.ds(to, 128), 128:256] = jnp.where(low, main, rim).astype(BF16)
+                field[c, pl.ds(at, 128), 0:128] = first.astype(BF16)
+                field[c, pl.ds(at, 128), 128:256] = jnp.where(low, main, rim).astype(BF16)
         return carry
 
-    lax.fori_loop(0, 8, fill, 0)
-    field[:, 0:16, :] = field[:, 1024:1040, :]
-    field[:, 1040:1056, :] = field[:, 16:32, :]
-    planes[...] = jnp.zeros_like(planes)
+    lax.fori_loop(0, 8, fill, 0, unroll=8)
+    field[:, NZ : NZ + 16, :] = field[:, 0:16, :]
+
+
+def sample_kernel(xt_ref, *rest):
+    refs, (out_ref, field, planes, yv, ot, tall) = (rest[0:3], rest[3:6]), rest[6:]
+    fill_field(refs, field)
     row = lax.broadcasted_iota(jnp.int32, (72, 512), 0)
     yv[...] = jnp.where(row < 64, row, jnp.where(row % 2 == 0, -1, 64)).astype(F32)
-    zv = (lax.broadcasted_iota(jnp.int32, (48, 512), 0) + 8).astype(F32)
-    part = lax.broadcasted_iota(jnp.int32, (8, 512), 0) // 2
-
-    def block(b, carry):
-        gx, gy, gz = (slot_row(xt_ref, r, b) for r in (R_GX, R_GY, R_GZ))
-        cy, cz = slot_row(xt_ref, R_CY, b), slot_row(xt_ref, R_CZ, b)
-        fall_x, fall_y, fall_z = gx < 0.0, gy < 0.0, gz < 0.0
-        wx = [jnp.maximum(-gx, 0.0), jnp.maximum(gx, 0.0), 1.0 - jnp.abs(gx)]
-        sx = [jnp.where(fall_x, -1.0, 0.0), jnp.where(fall_x, 0.0, 1.0), jnp.where(fall_x, 1.0, -1.0)]
-        places = yv[...]
-        wy = hat(places, cy + gy)
-        step_y = places - jnp.where(fall_y, cy - 1.0, cy)
-        sy = jnp.where(step_y == 0.0, -1.0, jnp.where(step_y == 1.0, 1.0, 0.0))
-        wx16, sx16 = ([a.astype(BF16) for a in ax] for ax in (wx, sx))
-        wy16, sy16 = wy[0:64].astype(BF16), sy[0:64].astype(BF16)
-        for s in range(3):
-            rows = slice(s * 64, s * 64 + 64)
-            planes[rows, 0:512] = (wx[s] * wy[0:64]).astype(BF16)
-            planes[rows, 512:1024] = sx16[s] * wy16
-            planes[rows, 1024:1536] = wx16[s] * sy16
-        for k, (ax, ay) in enumerate(((wx, wy), (sx, wy), (wx, sy))):
-            rim = jnp.where(
-                part == 0, ax[2], jnp.where(part == 1, ax[0], jnp.where(part == 2, ax[1], 0.0))
-            )
-            rim = jnp.concatenate([rim * ay[64:72], jnp.zeros((8, 512), F32)], axis=0)
-            planes[192:208, k * 512 : k * 512 + 512] = rim.astype(BF16)
+    zv = lax.broadcasted_iota(jnp.int32, (40, 512), 0).astype(F32)
+    ot[GRADS:, :] = jnp.zeros((LANES, TILES), F32)
+
+    def block(b, table):
+        write_planes(xt_ref, b, yv[...], table)
+        gz, cz = slot_row(xt_ref, R_GZ, b), slot_row(xt_ref, R_CZ, b)
         at = pl.multiple_of(b * ZB, ZB)
-        here = jnp.concatenate([field[c, pl.ds(at, 64), :] for c in range(CH)], axis=0)
-        wz = hat(zv, cz + gz + 16.0)
-        step_z = zv - jnp.where(fall_z, cz + 15.0, cz + 16.0)
+        here = jnp.concatenate([field[c, pl.ds(at, 48), :] for c in range(CH)], axis=0)
+        wz = hat(zv, cz + gz + 1.0)
+        step_z = zv - jnp.where(gz < 0.0, cz, cz + 1.0)
         sz = jnp.where(step_z == 0.0, -1.0, jnp.where(step_z == 1.0, 1.0, 0.0))
         masses = [slot_row(xt_ref, c, b) for c in range(CH)]
-        values = jnp.dot(here, planes[:, 0:512], preferred_element_type=F32)
         grads = []
-        slope_z = jnp.zeros((1, 512), F32)
-        for c in range(CH):
-            v = values[c * 64 + 8 : c * 64 + 56]
-            grads.append(jnp.sum(v * wz, axis=0, keepdims=True))
-            slope_z = slope_z + masses[c] * jnp.sum(v * sz, axis=0, keepdims=True)
-        for k in (1, 2):
-            slopes = jnp.dot(here, planes[:, k * 512 : k * 512 + 512], preferred_element_type=F32)
-            total = jnp.zeros((48, 512), F32)
+        for k in range(3):
+            sampled = jnp.dot(
+                here[:, 0:208], table[:, k * 512 : k * 512 + 512], preferred_element_type=F32
+            )
+            total = jnp.zeros((40, 512), F32)
             for c in range(CH):
-                total = total + masses[c] * slopes[c * 64 + 8 : c * 64 + 56]
-            grads.append(jnp.sum(total * wz, axis=0, keepdims=True))
+                v = sampled[c * 48 : c * 48 + 40]
+                if k == 0:
+                    grads.append(jnp.sum(v * wz, axis=0, keepdims=True))
+                total = total + masses[c] * v
+            if k == 0:
+                slope_z = jnp.sum(total * sz, axis=0, keepdims=True)
+            else:
+                grads.append(jnp.sum(total * wz, axis=0, keepdims=True))
         grads.append(slope_z)
         for r in range(7):
             ot[pl.ds(r * LANES + 2 * b, 1), :] = grads[r][:, 0:256]
             ot[pl.ds(r * LANES + 2 * b + 1, 1), :] = grads[r][:, 256:512]
+
+    def two(g, carry):
+        block(2 * g, planes.at[0])
+        block(2 * g + 1, planes.at[1])
         return carry
 
-    lax.fori_loop(0, NZ // ZB, block, 0, unroll=2)
-    ot[GRADS:, :] = jnp.zeros((LANES, TILES), F32)
+    lax.fori_loop(0, NZ // ZB // 2, two, 0)
     for j in range(BACK):
         for h in range(2):
             piece = ot[j * 128 : j * 128 + 128, h * 128 : h * 128 + 128]
@@ -431,6 +435,7 @@
     breadth = smoothing[:, None, None]
     k_row = correlation(breadth, ids[None, :256, None], ids[None, None, :])
     k_col = correlation(breadth, ids[None, :, None], ids[None, None, :256])
+    k_back = correlation(breadth, ids[None, :, None] - 1, ids[None, None, :256])
     rim = jnp.arange(128, dtype=jnp.int32)
     rim_y = (rim // 8 * TY - 1 + rim % 2 * (TY + 1)) % NY
     k_rim = correlation(smoothing[rim % 8 // 2][:, None], rim_y[:, None], ids[None, :])
@@ -442,10 +447,12 @@
         pack_kernel,
         shape((TILES * PAIRS, 128), BF16),
         [pltpu.VMEM((TILES * PAIRS + 16, 128), F32), mask],
-        12,
+        56,
     )(*split, table)
     arrived = exchange(records, PAIRS // 2, both)
-    arrived, k_row, k_col, k_rim = lax.optimization_barrier((arrived, k_row, k_col, k_rim))
+    arrived, k_row, k_col, k_back, k_rim = lax.optimization_barrier(
+        (arrived, k_row, k_col, k_back, k_rim)
+    )
     from_up = lax.ppermute(arrived, "slab", forth)
     from_dn = lax.ppermute(arrived, "slab", aft)
     turned = pltpu.VMEM((RECORD, TILES), F32)
@@ -474,26 +481,27 @@
         compiler_params=params(20),
     )(bias_values, lines, k_row, k_rim, observed[0], precision[0])
     lines = lax.all_to_all(lines, "pencil", split_axis=0, concat_axis=0, tiled=True)
-    field = call(
-        adjoint_kernel,
-        shape((2112, 128), BF16),
-        [pltpu.VMEM((CH, NZ, 128), BF16), pltpu.VMEM((CH, NZ, 128), F32)],
-        20,
-    )(lines, k_col)
-    field_up = lax.ppermute(field, "slab", forth)
-    field_dn = lax.ppermute(field, "slab", aft)
+    fields = []
+    for pair in range(2):
+        field = call(
+            functools.partial(adjoint_kernel, pair),
+            shape((NZ + 64, 128), BF16),
+            [pltpu.VMEM((2, NZ, 128), BF16), pltpu.VMEM((2, NZ, 128), F32)],
+            16,
+        )(lines, k_back)
+        fields += [field, lax.ppermute(field, "slab", forth), lax.ppermute(field, "slab", aft)]
     sampled = call(
         sample_kernel,
         shape((TILES * BACK, 128), BF16),
         [
-            pltpu.VMEM((CH, 1056, 256), BF16),
-            pltpu.VMEM((256, 1536), BF16),
+            pltpu.VMEM((CH, NZ + 16, 256), BF16),
+            pltpu.VMEM((2, 208, 1536), BF16),
             pltpu.VMEM((72, 512), F32),
             pltpu.VMEM((BACK * 128, TILES), F32),
             pltpu.VMEM((TILES * BACK + 8, 128), F32),
         ],
-        20,
-    )(xt, field, field_up, field_dn)
+        24,
+    )(xt, *fields)
     came_back = lax.all_to_all(
         sampled.reshape(TILES, BACK, 128), both, split_axis=0, concat_axis=0, tiled=True
     ).reshape(TILES * BACK, 128)

time: 146 us -> 137 us (0.938)
  Pallas kernels: 41.8 us -> 33.1 us
  blocking collectives: 49 us -> 52.1 us
  waiting for transfers between devices: 18.7 us -> 16.4 us
  other arithmetic: 7.61 us -> 9.82 us
  local copies, waits for them, and re-layouts: 5.04 us -> 3.08 us
    pallas_call x2 -> x3, Pallas kernels: 21.3 us -> 15.7 us  [the longest x1 12.1 us: per_device(): call(sample_kernel, shape((TILES * BACK, 128), BF16), [pltpu.VMEM((CH, NZ...]
    all_to_all x2, blocking collectives: 24.6 us -> 28.4 us  [per_device(): lax.all_to_all(lines, 'pencil', split_axis=0, concat_axis=0, tiled=True)]
    pallas_call x1, Pallas kernels: 11.6 us -> 8.12 us  [per_device(): call(forward_kernel, shape((N_PENCIL, CHUNK, 128), BF16), [pltpu.VMEM((CH...]
    all_to_all x1, waiting for transfers between devices: 9.31 us -> 7.09 us  [exchange(): rows = lax.all_to_all(rows, axes, split_axis=0, concat_axis=0, tiled=True)]
    unnamed x18 -> x12, local copies, waits for them, and re-layouts: 3.57 us -> 1.61 us
    ppermute x2 -> x4, waiting for transfers between devices: 7.33 us -> 5.42 us  [the longest x2 4.61 us: per_device(): lax.ppermute(field, 'slab', aft)]
    convert_element_type x3, other arithmetic: 3.48 us -> 5.22 us  [correlation(): return (profile + jnp.where(distance == 0.0, 1.0, 0.0)).astype(BF16)]
    ppermute x1, starting transfers between devices: 1.74 us -> 0.01 us  [per_device(): from_up = lax.ppermute(arrived, 'slab', forth)]
  transfers between devices with their start and end apart: 5 -> 7, of which waited for: 3 -> 6; matrix products, arithmetic and copies ran while one was open for 6% -> 8% of each run, Pallas kernels for 3% -> 4%
where the time goes in v2:
time: 137 us
  blocking collectives  52.1 us (38%)
  Pallas kernels  33.1 us (24%)
  starting transfers between devices  21.7 us (16%)
  waiting for transfers between devices  16.4 us (12%)
  other arithmetic  9.82 us (7%)
  local copies, waits for them, and re-layouts  3.08 us (2%)
    all_to_all x2, blocking collectives, per_device(): lax.all_to_all(lines, 'pencil', split_axis=0, concat_axis=0, tiled=True)  28.4 us
    all_to_all x1, blocking collectives, per_device(): lax.all_to_all(sampled.reshape(TILES, BACK, 128), both, split_axis=0, con...  23.7 us
    all_to_all x1, starting transfers between devices, exchange(): rows = lax.all_to_all(rows, axes, split_axis=0, concat_axis=0, tiled=True)  15.7 us
    pallas_call x1, Pallas kernels, per_device(): call(sample_kernel, shape((TILES * BACK, 128), BF16), [pltpu.VMEM((CH, NZ...  12.1 us
    pallas_call x1, Pallas kernels, per_device(): call(forward_kernel, shape((N_PENCIL, CHUNK, 128), BF16), [pltpu.VMEM((CH...  8.12 us
    all_to_all x1, waiting for transfers between devices, exchange(): rows = lax.all_to_all(rows, axes, split_axis=0, concat_axis=0, tiled=True)  7.09 us
    convert_element_type x3, other arithmetic, correlation(): return (profile + jnp.where(distance == 0.0, 1.0, 0.0)).astype(BF16)  5.22 us
    ppermute x2, starting transfers between devices, per_device(): lax.ppermute(field, 'slab', forth)  4.72 us
  transfers between devices with their start and end apart: 7, of which 6 were waited for; matrix products, arithmetic and copies ran while one was open for 8% of the time, Pallas kernels for 4%

profile of v2, /device:TPU:1, one launch (start us, length us, event | category | flops | bytes accessed | tf_op | source)
XLA Modules:
  0.0 137.0 jit_solution(12899936469629296535)
XLA Ops:
  0.6 2.8 %shard_map.95 = bf16[1536,128]{1,0:T(8,128)(2,1)} custom-call(f32[128,3,128]{2,1,0:T(4,128)} %bitcast.48, s32[128,3,128]{2,1,0:T(4,128)} %bitcast.49, bf16[128,4,128]{2,1,0:T(4,128)(2,1)} %bitcast.50, s32[32,256]{1,0:T(8,128)} %bitcast.44), custom_call_target="tpu_custom_call" | custom-call | tf_op jit(solution)/shard_map/pallas_call | solution.py:446
  3.4 15.7 %all-to-all-start = ((bf16[256,2,384]{2,1,0:T(2,128)(2,1)}), bf16[256,2,384]{2,1,0:T(2,128)(2,1)S(1)}, u32[]{:S(2)}, u32[]{:S(2)}) async-start(bf16[256,2,384]{2,1,0:T(2,128)(2,1)} %bitcast.46), calls=%async_computation | async-start | bytes 786432 | tf_op jit(solution)/shard_map/all_to_all | solution.py:419
  19.1 1.5 %fusion.32 = (f32[1]{0:T(128)}, f32[1]{0:T(128)}, f32[1]{0:T(128)}, f32[1]{0:T(128)}) fusion(f32[4]{0:T(128)} %param.12), kind=kLoop, calls=%fused_computation.63 | loop fusion | bytes 32 | tf_op jit(solution)/shard_map/gather | solution.py:441
  21.2 2.5 %multiply_multiply_fusion = (f32[128]{0:T(128)S(1)}, f32[128]{0:T(128)S(1)}) fusion(f32[]{:T(128)} %bitcast.17, f32[]{:T(128)} %bitcast.16, f32[]{:T(128)} %bitcast.15, f32[]{:T(128)} %bitcast.14), kind=kLoop, calls=%fused_computation.55 | loop fusion | flops 4096 | bytes 1040 | tf_op jit(solution)/shard_map/mul | solution.py:404
  25.6 2.7 %fusion.2 = (bf16[4,1024,256]{2,1,0:T(8,128)(2,1)S(1)}, bf16[4,1024,256]{2,1,0:T(8,128)(2,1)}) fusion(f32[1024,256]{1,0:T(8,128)S(1)} %get-tuple-element.23, f32[1024,256]{1,0:T(8,128)S(1)} %get-tuple-element.22, f32[4]{0:T(128)S(1)} %get-tuple-element.35, f32[4]{0:T(128)S(1)} %get-tuple-element.34, f32[1024,256]{1,0:T(8,128)S(1)} %get-tuple-element.27, ...), kind=kLoop, calls=%fused_computation.3 | loop fusion | flops 8388608 | bytes 8388640 | tf_op jit(solution)/shard_map/convert_element_type | solution.py:405
  28.3 2.2 %fusion.8.row_ref = bf16[4,256,1024]{2,1,0:T(8,128)(2,1)} fusion(f32[256,1024]{1,0:T(8,128)S(1)} %get-tuple-element.29, f32[4]{0:T(128)S(1)} %get-tuple-element.35, f32[4]{0:T(128)S(1)} %get-tuple-element.34, f32[256,1024]{1,0:T(8,128)S(1)} %get-tuple-element.28), kind=kLoop, calls=%fused_computation.11 | loop fusion | flops 4194304 | bytes 4194336 | tf_op jit(solution)/shard_map/convert_element_type | solution.py:405
  30.4 7.1 %all-to-all-done = bf16[256,2,384]{2,1,0:T(2,128)(2,1)S(1)} async-done(((bf16[256,2,384]{2,1,0:T(2,128)(2,1)}), bf16[256,2,384]{2,1,0:T(2,128)(2,1)S(1)}, u32[]{:S(2)}, u32[]{:S(2)}) %all-to-all-start) | async-done | bytes 393248 | tf_op jit(solution)/shard_map/all_to_all | solution.py:419
  38.0 3.0 %shard_map.96 = (f32[4,1040,128]{2,1,0:T(8,128)S(1)}, f32[768,256]{1,0:T(8,128)S(1)}) custom-call(bf16[1536,128]{1,0:T(8,128)(2,1)S(1)} %bitcast.39), custom_call_target="tpu_custom_call" | custom-call | tf_op jit(solution)/shard_map/pallas_call | solution.py:461
  41.0 1.2 collective-permute-done.up_ref
  42.2 2.7 %collective-permute-done.1.dn_ref = bf16[1536,128]{1,0:T(8,128)(2,1)S(1)} collective-permute-done((bf16[1536,128]{1,0:T(8,128)(2,1)S(1)}, bf16[1536,128]{1,0:T(8,128)(2,1)S(1)}, u32[]{:S(2)}, u32[]{:S(2)}) %collective-permute-start.1) | collective-permute-done | bytes 393248 | tf_op jit(solution)/shard_map/ppermute | solution.py:457
  44.9 1.6 %copy-done = bf16[4,1024,256]{2,1,0:T(8,128)(2,1)S(1)} copy-done((bf16[4,1024,256]{2,1,0:T(8,128)(2,1)S(1)}, bf16[4,1024,256]{2,1,0:T(8,128)(2,1)}, u32[]{:S(2)}) %copy-start) | copy-done | bytes 2097176
  46.5 8.1 %shard_map.97 = bf16[16,136,128]{2,1,0:T(8,128)(2,1)S(1)} custom-call(bf16[1536,128]{1,0:T(8,128)(2,1)S(1)} %collective-permute-done.up_ref, bf16[1536,128]{1,0:T(8,128)(2,1)S(1)} %collective-permute-done.1.dn_ref, f32[4,1040,128]{2,1,0:T(8,128)S(1)} %get-tuple-element.13.start_ref, bf16[4,1024,256]{2,1,0:T(8,128)(2,1)S(1)} %copy-done), custom_call_target="tpu_custom_call" | custom-call | tf_op jit(solution)/shard_map/pallas_call | solution.py:467
  54.7 14.8 %all_to_all.20.in_ref = bf16[16,136,128]{2,1,0:T(8,128)(2,1)S(1)} all-to-all(bf16[16,136,128]{2,1,0:T(8,128)(2,1)S(1)} %shard_map.97), channel_id=1, replica_groups=mesh['slab'=16,'pencil'=16] {'pencil'}, dimensions={0} | all-to-all | bytes 1114112 | tf_op jit(solution)/shard_map/all_to_all | solution.py:475
  69.5 2.2 %shard_map.98 = (bf16[64,1024]{1,0:T(8,128)(2,1)}, bf16[16,136,128]{2,1,0:T(8,128)(2,1)S(1)}) custom-call(f32[4]{0:T(128)S(1)} %copy-done.5, bf16[16,136,128]{2,1,0:T(8,128)(2,1)S(1)} %all_to_all.20.in_ref, bf16[4,256,1024]{2,1,0:T(8,128)(2,1)S(1)} %copy-done.1, bf16[128,1024]{1,0:T(8,128)(2,1)S(1)} %fusion.24.rim_ref, f32[64,1024]{1,0:T(8,128)S(1)} %bitcast.42, ...), custom_call_target="tpu_custom_call" | custom-call | tf_op jit(solution)/shard_map/pallas_call | solution.py:476
  71.7 13.6 %all_to_all.21.in_ref = bf16[16,136,128]{2,1,0:T(8,128)(2,1)S(1)} all-to-all(bf16[16,136,128]{2,1,0:T(8,128)(2,1)S(1)} %get-tuple-element.17), channel_id=1, replica_groups=mesh['slab'=16,'pencil'=16] {'pencil'}, dimensions={0} | all-to-all | bytes 1114112 | tf_op jit(solution)/shard_map/all_to_all | solution.py:483
  85.3 1.8 %shard_map.100.rest_3_ = bf16[1088,128]{1,0:T(8,128)(2,1)S(1)} custom-call(bf16[16,136,128]{2,1,0:T(8,128)(2,1)S(1)} %all_to_all.21.in_ref, bf16[4,1024,256]{2,1,0:T(8,128)(2,1)S(1)} %get-tuple-element.18.col_ref), custom_call_target="tpu_custom_call" | custom-call | tf_op jit(solution)/shard_map/pallas_call | solution.py:486
  87.1 3.0 %collective-permute-start.4 = (bf16[1088,128]{1,0:T(8,128)(2,1)S(1)}, bf16[1088,128]{1,0:T(8,128)(2,1)S(1)}, u32[]{:S(2)}, u32[]{:S(2)}) collective-permute-start(bf16[1088,128]{1,0:T(8,128)(2,1)S(1)} %shard_map.100.rest_3_), channel_id=1, source_target_pairs={{0,16},{16,32},{32,48},{48,64},{64,80},{80,96},{96,112},{112,128},... | collective-permute-start | bytes 835592 | tf_op jit(solution)/shard_map/ppermute | solution.py:492
  90.1 1.8 %shard_map.99.rest_0_ = bf16[1088,128]{1,0:T(8,128)(2,1)S(1)} custom-call(bf16[16,136,128]{2,1,0:T(8,128)(2,1)S(1)} %all_to_all.21.in_ref, bf16[4,1024,256]{2,1,0:T(8,128)(2,1)S(1)} %get-tuple-element.18.col_ref), custom_call_target="tpu_custom_call" | custom-call | tf_op jit(solution)/shard_map/pallas_call | solution.py:486
  91.9 1.8 %collective-permute-start.2 = (bf16[1088,128]{1,0:T(8,128)(2,1)S(1)}, bf16[1088,128]{1,0:T(8,128)(2,1)S(1)}, u32[]{:S(2)}, u32[]{:S(2)}) collective-permute-start(bf16[1088,128]{1,0:T(8,128)(2,1)S(1)} %shard_map.99.rest_0_), channel_id=1, source_target_pairs={{0,16},{16,32},{32,48},{48,64},{64,80},{80,96},{96,112},{112,128},... | collective-permute-start | bytes 835592 | tf_op jit(solution)/shard_map/ppermute | solution.py:492
  94.5 1.8 %collective-permute-done.5.rest_5_ = bf16[1088,128]{1,0:T(8,128)(2,1)S(1)} collective-permute-done((bf16[1088,128]{1,0:T(8,128)(2,1)S(1)}, bf16[1088,128]{1,0:T(8,128)(2,1)S(1)}, u32[]{:S(2)}, u32[]{:S(2)}) %collective-permute-start.5) | collective-permute-done | bytes 278560 | tf_op jit(solution)/shard_map/ppermute | solution.py:492
  97.1 2.8 %collective-permute-done.3.rest_2_ = bf16[1088,128]{1,0:T(8,128)(2,1)S(1)} collective-permute-done((bf16[1088,128]{1,0:T(8,128)(2,1)S(1)}, bf16[1088,128]{1,0:T(8,128)(2,1)S(1)}, u32[]{:S(2)}, u32[]{:S(2)}) %collective-permute-start.3) | collective-permute-done | bytes 278560 | tf_op jit(solution)/shard_map/ppermute | solution.py:492
  99.9 12.1 %shard_map.101 = bf16[1024,128]{1,0:T(8,128)(2,1)S(1)} custom-call(f32[768,256]{1,0:T(8,128)S(1)} %get-tuple-element.12.xt_ref, bf16[1088,128]{1,0:T(8,128)(2,1)S(1)} %shard_map.99.rest_0_, bf16[1088,128]{1,0:T(8,128)(2,1)S(1)} %collective-permute-done.2.rest_1_, bf16[1088,128]{1,0:T(8,128)(2,1)S(1)} %collective-permute-done.3.rest_2_, ...), custom_call_target="tpu_custom_call" | custom-call | tf_op jit(solution)/shard_map/pallas_call | solution.py:493
  112.0 23.7 %all_to_all.22 = bf16[256,4,128]{2,1,0:T(4,128)(2,1)S(1)} all-to-all(bf16[256,4,128]{2,1,0:T(4,128)(2,1)S(1)} %bitcast.41), channel_id=1, replica_groups=mesh['slab'=16,'pencil'=16] {'slab','pencil'}, dimensions={0} | all-to-all | bytes 524288 | tf_op jit(solution)/shard_map/all_to_all | solution.py:505
  135.7 1.3 shard_map.102
  (26 shorter events, 4.7 us)
Async XLA Ops:
  3.4 34.1 %all-to-all-start = ((bf16[256,2,384]{2,1,0:T(2,128)(2,1)}), bf16[256,2,384]{2,1,0:T(2,128)(2,1)S(1)}, u32[]{:S(2)}, u32[]{:S(2)}) async-start(bf16[256,2,384]{2,1,0:T(2,128)(2,1)} %bitcast.46), calls=%async_computation | async-start | bytes 786432 | tf_op jit(solution)/shard_map/all_to_all | solution.py:419
  37.5 4.7 %collective-permute-start = (bf16[1536,128]{1,0:T(8,128)(2,1)S(1)}, bf16[1536,128]{1,0:T(8,128)(2,1)S(1)}, u32[]{:S(2)}, u32[]{:S(2)}) collective-permute-start(bf16[1536,128]{1,0:T(8,128)(2,1)S(1)} %bitcast.37), channel_id=1, source_target_pairs={{0,16},{16,32},{32,48},{48,64},{64,80},{80,96},{96,112},{112,128},... | collective-permute-start | bytes 1179656 | tf_op jit(solution)/shard_map/ppermute | solution.py:456
  37.5 7.4 %collective-permute-start.1 = (bf16[1536,128]{1,0:T(8,128)(2,1)S(1)}, bf16[1536,128]{1,0:T(8,128)(2,1)S(1)}, u32[]{:S(2)}, u32[]{:S(2)}) collective-permute-start(bf16[1536,128]{1,0:T(8,128)(2,1)S(1)} %bitcast.38), channel_id=1, source_target_pairs={{16,0},{32,16},{48,32},{64,48},{80,64},{96,80},{112,96},{128,112},... | collective-permute-start | bytes 1179656 | tf_op jit(solution)/shard_map/ppermute | solution.py:457
  44.9 1.6 %copy-start = (bf16[4,1024,256]{2,1,0:T(8,128)(2,1)S(1)}, bf16[4,1024,256]{2,1,0:T(8,128)(2,1)}, u32[]{:S(2)}) copy-start(bf16[4,1024,256]{2,1,0:T(8,128)(2,1)} %get-tuple-element.14.col_ref) | copy-start | bytes 6291460
  46.5 22.9 %copy-start.1 = (bf16[4,256,1024]{2,1,0:T(8,128)(2,1)S(1)}, bf16[4,256,1024]{2,1,0:T(8,128)(2,1)}, u32[]{:S(2)}) copy-start(bf16[4,256,1024]{2,1,0:T(8,128)(2,1)} %fusion.8.row_ref) | copy-start | bytes 6291460
  46.5 22.9 %copy-start.2 = (f32[1,64,1024]{2,1,0:T(8,128)S(1)}, f32[1,64,1024]{2,1,0:T(8,128)}, u32[]{:S(2)}) copy-start(f32[1,64,1024]{2,1,0:T(8,128)} %param.14) | copy-start | bytes 786436
  46.5 22.9 %copy-start.3 = (f32[1,64,1024]{2,1,0:T(8,128)S(1)}, f32[1,64,1024]{2,1,0:T(8,128)}, u32[]{:S(2)}) copy-start(f32[1,64,1024]{2,1,0:T(8,128)} %param.15) | copy-start | bytes 786436
  46.5 22.9 %copy-start.5 = (f32[4]{0:T(128)S(1)}, f32[4]{0:T(128)}, u32[]{:S(2)}) copy-start(f32[4]{0:T(128)} %bias_ref.1) | copy-start | bytes 52
  87.1 7.4 %collective-permute-start.4 = (bf16[1088,128]{1,0:T(8,128)(2,1)S(1)}, bf16[1088,128]{1,0:T(8,128)(2,1)S(1)}, u32[]{:S(2)}, u32[]{:S(2)}) collective-permute-start(bf16[1088,128]{1,0:T(8,128)(2,1)S(1)} %shard_map.100.rest_3_), channel_id=1, source_target_pairs={{0,16},{16,32},{32,48},{48,64},{64,80},{80,96},{96,112},{112,128},... | collective-permute-start | bytes 835592 | tf_op jit(solution)/shard_map/ppermute | solution.py:492
  90.0 6.3 %collective-permute-start.5 = (bf16[1088,128]{1,0:T(8,128)(2,1)S(1)}, bf16[1088,128]{1,0:T(8,128)(2,1)S(1)}, u32[]{:S(2)}, u32[]{:S(2)}) collective-permute-start(bf16[1088,128]{1,0:T(8,128)(2,1)S(1)} %shard_map.100.rest_3_), channel_id=1, source_target_pairs={{16,0},{32,16},{48,32},{64,48},{80,64},{96,80},{112,96},{128,112},... | collective-permute-start | bytes 835592 | tf_op jit(solution)/shard_map/ppermute | solution.py:492
  91.9 43.8 %copy-start.4 = (s32[1,256,32]{1,2,0:T(8,128)S(1)}, s32[1,256,32]{1,2,0:T(8,128)}, u32[]{:S(2)}) copy-start(s32[1,256,32]{1,2,0:T(8,128)} %param.11) | copy-start | bytes 98308
  91.9 5.3 %collective-permute-start.2 = (bf16[1088,128]{1,0:T(8,128)(2,1)S(1)}, bf16[1088,128]{1,0:T(8,128)(2,1)S(1)}, u32[]{:S(2)}, u32[]{:S(2)}) collective-permute-start(bf16[1088,128]{1,0:T(8,128)(2,1)S(1)} %shard_map.99.rest_0_), channel_id=1, source_target_pairs={{0,16},{16,32},{32,48},{48,64},{64,80},{80,96},{96,112},{112,128},... | collective-permute-start | bytes 835592 | tf_op jit(solution)/shard_map/ppermute | solution.py:492
  93.6 6.3 %collective-permute-start.3 = (bf16[1088,128]{1,0:T(8,128)(2,1)S(1)}, bf16[1088,128]{1,0:T(8,128)(2,1)S(1)}, u32[]{:S(2)}, u32[]{:S(2)}) collective-permute-start(bf16[1088,128]{1,0:T(8,128)(2,1)S(1)} %shard_map.99.rest_0_), channel_id=1, source_target_pairs={{16,0},{32,16},{48,32},{64,48},{80,64},{96,80},{112,96},{128,112},... | collective-permute-start | bytes 835592 | tf_op jit(solution)/shard_map/ppermute | solution.py:492

commit v3 on v2

--- a/solution.py
+++ b/solution.py
@@ -183,7 +183,9 @@
     return table.T[0:8]
 
 
-def forward_kernel(up_ref, dn_ref, start_ref, col_ref, out_ref, acc, xt, wide, yv, zv, dens, smooth):
+def forward_kernel(up_ref, dn_ref, start_ref, col_ref, out_ref, acc, xt, wide, yv, zv, dens, smooth, cols, sem):
+    fetch = pltpu.make_async_copy(col_ref, cols, sem)
+    fetch.start()
     fill_places(yv, zv)
     acc[...] = start_ref[...]
     transpose_records(up_ref, wide, xt)
@@ -193,7 +195,8 @@
     acc[:, NZ : NZ + 1, :] += acc[:, 0:1, :]
     acc[:, 1:2, :] += acc[:, NZ + 1 : NZ + 2, :]
     dens[...] = acc[:, 1 : NZ + 1, :].astype(BF16)
-    along_z(dens, col_ref, smooth, 0, CH)
+    fetch.wait()
+    along_z(dens, cols, smooth, 0, CH)
     low = lanes_of((64, 128)) < LANES
 
     def send(p, carry):
@@ -314,6 +317,17 @@
         planes[192:208, k * 512 : k * 512 + 512] = rim.astype(BF16)
 
 
+def weights_kernel(xt_ref, planes, yv):
+    row = lax.broadcasted_iota(jnp.int32, (72, 512), 0)
+    yv[...] = jnp.where(row < 64, row, jnp.where(row % 2 == 0, -1, 64)).astype(F32)
+
+    def block(b, carry):
+        write_planes(xt_ref, b, yv[...], planes.at[b])
+        return carry
+
+    lax.fori_loop(0, NZ // ZB, block, 0, unroll=2)
+
+
 def fill_field(refs, field):
     lane = lanes_of((128, 128))
     low = lane < LANES
@@ -347,16 +361,13 @@
     field[:, NZ : NZ + 16, :] = field[:, 0:16, :]
 
 
-def sample_kernel(xt_ref, *rest):
-    refs, (out_ref, field, planes, yv, ot, tall) = (rest[0:3], rest[3:6]), rest[6:]
+def sample_kernel(planes, xt_ref, *rest):
+    refs, (out_ref, field, ot, tall) = (rest[0:3], rest[3:6]), rest[6:]
     fill_field(refs, field)
-    row = lax.broadcasted_iota(jnp.int32, (72, 512), 0)
-    yv[...] = jnp.where(row < 64, row, jnp.where(row % 2 == 0, -1, 64)).astype(F32)
     zv = lax.broadcasted_iota(jnp.int32, (40, 512), 0).astype(F32)
     ot[GRADS:, :] = jnp.zeros((LANES, TILES), F32)
 
-    def block(b, table):
-        write_planes(xt_ref, b, yv[...], table)
+    def block(b, carry):
         gz, cz = slot_row(xt_ref, R_GZ, b), slot_row(xt_ref, R_CZ, b)
         at = pl.multiple_of(b * ZB, ZB)
         here = jnp.concatenate([field[c, pl.ds(at, 48), :] for c in range(CH)], axis=0)
@@ -367,7 +378,7 @@
         grads = []
         for k in range(3):
             sampled = jnp.dot(
-                here[:, 0:208], table[:, k * 512 : k * 512 + 512], preferred_element_type=F32
+                here[:, 0:208], planes[b, :, k * 512 : k * 512 + 512], preferred_element_type=F32
             )
             total = jnp.zeros((40, 512), F32)
             for c in range(CH):
@@ -383,13 +394,9 @@
         for r in range(7):
             ot[pl.ds(r * LANES + 2 * b, 1), :] = grads[r][:, 0:256]
             ot[pl.ds(r * LANES + 2 * b + 1, 1), :] = grads[r][:, 256:512]
-
-    def two(g, carry):
-        block(2 * g, planes.at[0])
-        block(2 * g + 1, planes.at[1])
-        return carry
-
-    lax.fori_loop(0, NZ // ZB // 2, two, 0)
+        return carry
+
+    lax.fori_loop(0, NZ // ZB, block, 0, unroll=2)
     for j in range(BACK):
         for h in range(2):
             piece = ot[j * 128 : j * 128 + 128, h * 128 : h * 128 + 128]
@@ -464,14 +471,21 @@
         [wide] + places,
         12,
     )(arrived)
-    lines = call(
+    whole = pl.BlockSpec(memory_space=pltpu.VMEM)
+    lines = pl.pallas_call(
         forward_kernel,
-        shape((N_PENCIL, CHUNK, 128), BF16),
-        [pltpu.VMEM((CH, 1040, 128), F32), turned, wide]
+        out_shape=shape((N_PENCIL, CHUNK, 128), BF16),
+        in_specs=[whole] * 3 + [pl.BlockSpec(memory_space=pltpu.HBM)],
+        scratch_shapes=[pltpu.VMEM((CH, 1040, 128), F32), turned, wide]
         + places
-        + [pltpu.VMEM((CH, NZ, 128), BF16), pltpu.VMEM((CH, NZ, 128), F32)],
-        24,
-    )(from_up, from_dn, acc, k_col)
+        + [
+            pltpu.VMEM((CH, NZ, 128), BF16),
+            pltpu.VMEM((CH, NZ, 128), F32),
+            pltpu.VMEM((CH, NZ, 256), BF16),
+            pltpu.SemaphoreType.DMA,
+        ],
+        compiler_params=params(24),
+    )(from_up, from_dn, acc, pltpu.with_memory_space_constraint(k_col, pltpu.HBM))
     lines = lax.all_to_all(lines, "pencil", split_axis=0, concat_axis=0, tiled=True)
     model_field, lines = pl.pallas_call(
         lines_kernel,
@@ -489,19 +503,26 @@
             [pltpu.VMEM((2, NZ, 128), BF16), pltpu.VMEM((2, NZ, 128), F32)],
             16,
         )(lines, k_back)
+        if pair == 1:
+            field, late = lax.optimization_barrier((field, xt))
         fields += [field, lax.ppermute(field, "slab", forth), lax.ppermute(field, "slab", aft)]
+    planes = pl.pallas_call(
+        weights_kernel,
+        out_shape=shape((NZ // ZB, 208, 1536), BF16),
+        scratch_shapes=[pltpu.VMEM((72, 512), F32)],
+        compiler_params=params(22),
+        cost_estimate=pl.CostEstimate(flops=60_000_000, bytes_accessed=21_000_000, transcendentals=0),
+    )(late)
     sampled = call(
         sample_kernel,
         shape((TILES * BACK, 128), BF16),
         [
             pltpu.VMEM((CH, NZ + 16, 256), BF16),
-            pltpu.VMEM((2, 208, 1536), BF16),
-            pltpu.VMEM((72, 512), F32),
             pltpu.VMEM((BACK * 128, TILES), F32),
             pltpu.VMEM((TILES * BACK + 8, 128), F32),
         ],
-        24,
-    )(xt, *fields)
+        30,
+    )(planes, xt, *fields)
     came_back = lax.all_to_all(
         sampled.reshape(TILES, BACK, 128), both, split_axis=0, concat_axis=0, tiled=True
     ).reshape(TILES * BACK, 128)

time: 137 us -> 132 us (0.964)
  waiting for transfers between devices: 16.4 us -> 10 us
  starting transfers between devices: 21.7 us -> 24.7 us
  blocking collectives: 52.1 us -> 49.7 us
  Pallas kernels: 33.1 us -> 34.9 us
  local copies, waits for them, and re-layouts: 3.08 us -> 1.46 us
    ppermute x2, starting transfers between devices: 0.85 us -> 5.43 us  [per_device(): lax.ppermute(field, 'slab', aft)]
    ppermute x2, waiting for transfers between devices: 4.61 us -> 0.12 us  [per_device(): lax.ppermute(field, 'slab', aft)]
    pallas_call x1 -> x2, Pallas kernels: 8.12 us -> 12.2 us  [the longest x1 8.14 us: per_device(): pl.pallas_call(forward_kernel, out_shape=shape((N_PENCIL, CHUNK, 128), BF...]
    all_to_all x2, blocking collectives: 28.4 us -> 24.3 us  [per_device(): lax.all_to_all(lines, 'pencil', split_axis=0, concat_axis=0, tiled=True)]
    ppermute x2, starting transfers between devices: 4.72 us -> 1.87 us  [per_device(): lax.ppermute(field, 'slab', forth)]
    pallas_call x1, Pallas kernels: 12.1 us -> 9.72 us  [per_device(): call(sample_kernel, shape((TILES * BACK, 128), BF16), [pltpu.VMEM((CH, NZ...]
    ppermute x1, starting transfers between devices: 0.01 us -> 1.74 us  [per_device(): from_up = lax.ppermute(arrived, 'slab', forth)]
    all_to_all x1, blocking collectives: 23.7 us -> 25.3 us  [per_device(): lax.all_to_all(sampled.reshape(TILES, BACK, 128), both, split_axis=0, con...]
  transfers between devices with their start and end apart: 7 -> 7, of which waited for: 6 -> 3; matrix products, arithmetic and copies ran while one was open for 8% -> 9% of each run, Pallas kernels for 4% -> 7%
where the time goes in v3:
time: 132 us; the launch traced here: 131 us
  blocking collectives  49.7 us (38%)
  Pallas kernels  34.9 us (26%)
  starting transfers between devices  24.7 us (19%)
  waiting for transfers between devices  10 us (8%)
  other arithmetic  9.78 us (7%)
  local copies, waits for them, and re-layouts  1.46 us (1%)
    all_to_all x1, blocking collectives, per_device(): lax.all_to_all(sampled.reshape(TILES, BACK, 128), both, split_axis=0, con...  25.3 us
    all_to_all x2, blocking collectives, per_device(): lax.all_to_all(lines, 'pencil', split_axis=0, concat_axis=0, tiled=True)  24.3 us
    all_to_all x1, starting transfers between devices, exchange(): rows = lax.all_to_all(rows, axes, split_axis=0, concat_axis=0, tiled=True)  15.7 us
    pallas_call x1, Pallas kernels, per_device(): call(sample_kernel, shape((TILES * BACK, 128), BF16), [pltpu.VMEM((CH, NZ...  9.72 us
    pallas_call x1, Pallas kernels, per_device(): pl.pallas_call(forward_kernel, out_shape=shape((N_PENCIL, CHUNK, 128), BF...  8.14 us
    all_to_all x1, waiting for transfers between devices, exchange(): rows = lax.all_to_all(rows, axes, split_axis=0, concat_axis=0, tiled=True)  7.16 us
    ppermute x2, starting transfers between devices, per_device(): lax.ppermute(field, 'slab', aft)  5.43 us
    convert_element_type x3, other arithmetic, correlation(): return (profile + jnp.where(distance == 0.0, 1.0, 0.0)).astype(BF16)  5.24 us
  transfers between devices with their start and end apart: 7, of which 3 were waited for; matrix products, arithmetic and copies ran while one was open for 9% of the time, Pallas kernels for 7%

profile of v3, /device:TPU:1, one launch (start us, length us, event | category | flops | bytes accessed | tf_op | source)
XLA Modules:
  0.0 131.3 jit_solution(10545073387511343639)
XLA Ops:
  0.6 2.8 %shard_map.95 = bf16[1536,128]{1,0:T(8,128)(2,1)} custom-call(f32[128,3,128]{2,1,0:T(4,128)} %bitcast.48, s32[128,3,128]{2,1,0:T(4,128)} %bitcast.49, bf16[128,4,128]{2,1,0:T(4,128)(2,1)} %bitcast.50, s32[32,256]{1,0:T(8,128)} %bitcast.44), custom_call_target="tpu_custom_call" | custom-call | tf_op jit(solution)/shard_map/pallas_call | solution.py:453
  3.4 15.7 %all-to-all-start = ((bf16[256,2,384]{2,1,0:T(2,128)(2,1)}), bf16[256,2,384]{2,1,0:T(2,128)(2,1)S(1)}, u32[]{:S(2)}, u32[]{:S(2)}) async-start(bf16[256,2,384]{2,1,0:T(2,128)(2,1)} %bitcast.46), calls=%async_computation | async-start | bytes 786432 | tf_op jit(solution)/shard_map/all_to_all | solution.py:426
  19.7 1.4 %fusion.32 = (f32[1]{0:T(128)}, f32[1]{0:T(128)}, f32[1]{0:T(128)}, f32[1]{0:T(128)}) fusion(f32[4]{0:T(128)} %param.12), kind=kLoop, calls=%fused_computation.63 | loop fusion | bytes 32 | tf_op jit(solution)/shard_map/gather | solution.py:448
  21.2 2.5 %multiply_multiply_fusion = (f32[128]{0:T(128)S(1)}, f32[128]{0:T(128)S(1)}) fusion(f32[]{:T(128)} %bitcast.17, f32[]{:T(128)} %bitcast.16, f32[]{:T(128)} %bitcast.15, f32[]{:T(128)} %bitcast.14), kind=kLoop, calls=%fused_computation.55 | loop fusion | flops 4096 | bytes 1040 | tf_op jit(solution)/shard_map/mul | solution.py:411
  24.2 0.9 negate_multiply_fusion
  25.5 2.7 %fusion.2 = (bf16[4,1024,256]{2,1,0:T(8,128)(2,1)S(1)}, bf16[4,1024,256]{2,1,0:T(8,128)(2,1)}) fusion(f32[1024,256]{1,0:T(8,128)S(1)} %get-tuple-element.27, f32[1024,256]{1,0:T(8,128)S(1)} %get-tuple-element.26, f32[4]{0:T(128)S(1)} %get-tuple-element.39, f32[4]{0:T(128)S(1)} %get-tuple-element.38, f32[1024,256]{1,0:T(8,128)S(1)} %get-tuple-element.31, ...), kind=kLoop, calls=%fused_computation.3 | loop fusion | flops 8388608 | bytes 8388640 | tf_op jit(solution)/shard_map/convert_element_type | solution.py:412
  28.2 2.2 %fusion.8.row_ref = bf16[4,256,1024]{2,1,0:T(8,128)(2,1)} fusion(f32[256,1024]{1,0:T(8,128)S(1)} %get-tuple-element.33, f32[4]{0:T(128)S(1)} %get-tuple-element.39, f32[4]{0:T(128)S(1)} %get-tuple-element.38, f32[256,1024]{1,0:T(8,128)S(1)} %get-tuple-element.32), kind=kLoop, calls=%fused_computation.11 | loop fusion | flops 4194304 | bytes 4194336 | tf_op jit(solution)/shard_map/convert_element_type | solution.py:412
  30.3 7.2 %all-to-all-done = bf16[256,2,384]{2,1,0:T(2,128)(2,1)S(1)} async-done(((bf16[256,2,384]{2,1,0:T(2,128)(2,1)}), bf16[256,2,384]{2,1,0:T(2,128)(2,1)S(1)}, u32[]{:S(2)}, u32[]{:S(2)}) %all-to-all-start) | async-done | bytes 393248 | tf_op jit(solution)/shard_map/all_to_all | solution.py:426
  37.5 1.7 %collective-permute-start = (bf16[1536,128]{1,0:T(8,128)(2,1)S(1)}, bf16[1536,128]{1,0:T(8,128)(2,1)S(1)}, u32[]{:S(2)}, u32[]{:S(2)}) collective-permute-start(bf16[1536,128]{1,0:T(8,128)(2,1)S(1)} %bitcast.38), channel_id=1, source_target_pairs={{0,16},{16,32},{32,48},{48,64},{64,80},{80,96},{96,112},{112,128},... | collective-permute-start | bytes 1179656 | tf_op jit(solution)/shard_map/ppermute | solution.py:463
  39.2 3.0 %shard_map.96 = (f32[4,1040,128]{2,1,0:T(8,128)S(1)}, f32[768,256]{1,0:T(8,128)S(1)}) custom-call(bf16[1536,128]{1,0:T(8,128)(2,1)S(1)} %bitcast.39), custom_call_target="tpu_custom_call" | custom-call | tf_op jit(solution)/shard_map/pallas_call | solution.py:468
  42.3 2.7 %collective-permute-done.1.dn_ref = bf16[1536,128]{1,0:T(8,128)(2,1)S(1)} collective-permute-done((bf16[1536,128]{1,0:T(8,128)(2,1)S(1)}, bf16[1536,128]{1,0:T(8,128)(2,1)S(1)}, u32[]{:S(2)}, u32[]{:S(2)}) %collective-permute-start.1) | collective-permute-done | bytes 393248 | tf_op jit(solution)/shard_map/ppermute | solution.py:464
  45.0 8.1 %shard_map.97 = bf16[16,136,128]{2,1,0:T(8,128)(2,1)S(1)} custom-call(bf16[1536,128]{1,0:T(8,128)(2,1)S(1)} %collective-permute-done.up_ref, bf16[1536,128]{1,0:T(8,128)(2,1)S(1)} %collective-permute-done.1.dn_ref, f32[4,1040,128]{2,1,0:T(8,128)S(1)} %get-tuple-element.14.start_ref, bf16[4,1024,256]{2,1,0:T(8,128)(2,1)} %get-tuple-element.15.col_ref), custom_call_target="tpu_custom_call" | custom-call | tf_op jit(solution)/shard_map/pallas_call | solution.py:475
  53.1 12.1 %all_to_all.20.in_ref = bf16[16,136,128]{2,1,0:T(8,128)(2,1)S(1)} all-to-all(bf16[16,136,128]{2,1,0:T(8,128)(2,1)S(1)} %shard_map.97), channel_id=1, replica_groups=mesh['slab'=16,'pencil'=16] {'pencil'}, dimensions={0} | all-to-all | bytes 1114112 | tf_op jit(solution)/shard_map/all_to_all | solution.py:489
  65.3 2.2 %shard_map.98 = (bf16[64,1024]{1,0:T(8,128)(2,1)}, bf16[16,136,128]{2,1,0:T(8,128)(2,1)S(1)}) custom-call(f32[4]{0:T(128)S(1)} %copy-done.4, bf16[16,136,128]{2,1,0:T(8,128)(2,1)S(1)} %all_to_all.20.in_ref, bf16[4,256,1024]{2,1,0:T(8,128)(2,1)S(1)} %copy-done, bf16[128,1024]{1,0:T(8,128)(2,1)S(1)} %fusion.24.rim_ref, f32[64,1024]{1,0:T(8,128)S(1)} %bitcast.42, ...), custom_call_target="tpu_custom_call" | custom-call | tf_op jit(solution)/shard_map/pallas_call | solution.py:490
  67.5 12.2 %all_to_all.21.in_ref = bf16[16,136,128]{2,1,0:T(8,128)(2,1)S(1)} all-to-all(bf16[16,136,128]{2,1,0:T(8,128)(2,1)S(1)} %get-tuple-element.18), channel_id=1, replica_groups=mesh['slab'=16,'pencil'=16] {'pencil'}, dimensions={0} | all-to-all | bytes 1114112 | tf_op jit(solution)/shard_map/all_to_all | solution.py:497
  79.7 1.8 %shard_map.99.rest_3_ = bf16[1088,128]{1,0:T(8,128)(2,1)S(1)} custom-call(bf16[16,136,128]{2,1,0:T(8,128)(2,1)S(1)} %all_to_all.21.in_ref, bf16[4,1024,256]{2,1,0:T(8,128)(2,1)S(1)} %get-tuple-element.19.col_ref), custom_call_target="tpu_custom_call" | custom-call | tf_op jit(solution)/shard_map/pallas_call | solution.py:500
  81.5 4.9 %collective-permute-start.5 = (bf16[1088,128]{1,0:T(8,128)(2,1)S(1)}, bf16[1088,128]{1,0:T(8,128)(2,1)S(1)}, u32[]{:S(2)}, u32[]{:S(2)}) collective-permute-start(bf16[1088,128]{1,0:T(8,128)(2,1)S(1)} %shard_map.99.rest_3_), channel_id=1, source_target_pairs={{16,0},{32,16},{48,32},{64,48},{80,64},{96,80},{112,96},{128,112},... | collective-permute-start | bytes 835592 | tf_op jit(solution)/shard_map/ppermute | solution.py:508
  86.4 0.7 collective-permute-start.4
  87.1 1.8 %shard_map.101.rest_0_ = bf16[1088,128]{1,0:T(8,128)(2,1)S(1)} custom-call(bf16[16,136,128]{2,1,0:T(8,128)(2,1)S(1)} %all_to_all.21.in_ref, bf16[4,1024,256]{2,1,0:T(8,128)(2,1)S(1)} %get-tuple-element.19.col_ref), custom_call_target="tpu_custom_call" | custom-call | tf_op jit(solution)/shard_map/pallas_call | solution.py:500
  89.5 1.2 collective-permute-start.2
  90.6 4.1 %shard_map.100.planes = bf16[32,208,1536]{2,1,0:T(8,128)(2,1)S(1)} custom-call(f32[768,256]{1,0:T(8,128)S(1)} %get-tuple-element.21.xt_ref), custom_call_target="tpu_custom_call" | custom-call | flops 60000000 | bytes 21000000 | tf_op jit(solution)/shard_map/pallas_call | solution.py:509
  94.9 9.7 %shard_map.102 = bf16[1024,128]{1,0:T(8,128)(2,1)S(1)} custom-call(bf16[32,208,1536]{2,1,0:T(8,128)(2,1)S(1)} %shard_map.100.planes, f32[768,256]{1,0:T(8,128)S(1)} %get-tuple-element.21.xt_ref, bf16[1088,128]{1,0:T(8,128)(2,1)S(1)} %shard_map.101.rest_0_, bf16[1088,128]{1,0:T(8,128)(2,1)S(1)} %collective-permute-done.2.rest_1_, ...), custom_call_target="tpu_custom_call" | custom-call | tf_op jit(solution)/shard_map/pallas_call | solution.py:516
  104.6 25.3 %all_to_all.22 = bf16[256,4,128]{2,1,0:T(4,128)(2,1)S(1)} all-to-all(bf16[256,4,128]{2,1,0:T(4,128)(2,1)S(1)} %bitcast.40), channel_id=1, replica_groups=mesh['slab'=16,'pencil'=16] {'slab','pencil'}, dimensions={0} | all-to-all | bytes 524288 | tf_op jit(solution)/shard_map/all_to_all | solution.py:526
  130.0 1.3 %shard_map.103 = f32[128,7,128]{2,1,0:T(8,128)} custom-call(bf16[1024,128]{1,0:T(8,128)(2,1)S(1)} %bitcast.41, s32[32,256]{1,0:T(8,128)S(1)} %bitcast.45), custom_call_target="tpu_custom_call" | custom-call | tf_op jit(solution)/shard_map/pallas_call | solution.py:529
  (25 shorter events, 2.3 us)
Async XLA Ops:
  3.4 34.1 %all-to-all-start = ((bf16[256,2,384]{2,1,0:T(2,128)(2,1)}), bf16[256,2,384]{2,1,0:T(2,128)(2,1)S(1)}, u32[]{:S(2)}, u32[]{:S(2)}) async-start(bf16[256,2,384]{2,1,0:T(2,128)(2,1)} %bitcast.46), calls=%async_computation | async-start | bytes 786432 | tf_op jit(solution)/shard_map/all_to_all | solution.py:426
  30.3 35.0 %copy-start.1 = (f32[1,64,1024]{2,1,0:T(8,128)S(1)}, f32[1,64,1024]{2,1,0:T(8,128)}, u32[]{:S(2)}) copy-start(f32[1,64,1024]{2,1,0:T(8,128)} %param.14) | copy-start | bytes 786436
  30.3 35.0 %copy-start.2 = (f32[1,64,1024]{2,1,0:T(8,128)S(1)}, f32[1,64,1024]{2,1,0:T(8,128)}, u32[]{:S(2)}) copy-start(f32[1,64,1024]{2,1,0:T(8,128)} %param.15) | copy-start | bytes 786436
  30.3 35.0 %copy-start.4 = (f32[4]{0:T(128)S(1)}, f32[4]{0:T(128)}, u32[]{:S(2)}) copy-start(f32[4]{0:T(128)} %bias_ref.1) | copy-start | bytes 52
  37.5 27.8 %copy-start = (bf16[4,256,1024]{2,1,0:T(8,128)(2,1)S(1)}, bf16[4,256,1024]{2,1,0:T(8,128)(2,1)}, u32[]{:S(2)}) copy-start(bf16[4,256,1024]{2,1,0:T(8,128)(2,1)} %fusion.8.row_ref) | copy-start | bytes 6291460
  37.5 7.5 %collective-permute-start.1 = (bf16[1536,128]{1,0:T(8,128)(2,1)S(1)}, bf16[1536,128]{1,0:T(8,128)(2,1)S(1)}, u32[]{:S(2)}, u32[]{:S(2)}) collective-permute-start(bf16[1536,128]{1,0:T(8,128)(2,1)S(1)} %bitcast.37), channel_id=1, source_target_pairs={{16,0},{32,16},{48,32},{64,48},{80,64},{96,80},{112,96},{128,112},... | collective-permute-start | bytes 1179656 | tf_op jit(solution)/shard_map/ppermute | solution.py:464
  37.5 7.5 %collective-permute-start = (bf16[1536,128]{1,0:T(8,128)(2,1)S(1)}, bf16[1536,128]{1,0:T(8,128)(2,1)S(1)}, u32[]{:S(2)}, u32[]{:S(2)}) collective-permute-start(bf16[1536,128]{1,0:T(8,128)(2,1)S(1)} %bitcast.38), channel_id=1, source_target_pairs={{0,16},{16,32},{32,48},{48,64},{64,80},{80,96},{96,112},{112,128},... | collective-permute-start | bytes 1179656 | tf_op jit(solution)/shard_map/ppermute | solution.py:463
  81.5 13.2 %collective-permute-start.5 = (bf16[1088,128]{1,0:T(8,128)(2,1)S(1)}, bf16[1088,128]{1,0:T(8,128)(2,1)S(1)}, u32[]{:S(2)}, u32[]{:S(2)}) collective-permute-start(bf16[1088,128]{1,0:T(8,128)(2,1)S(1)} %shard_map.99.rest_3_), channel_id=1, source_target_pairs={{16,0},{32,16},{48,32},{64,48},{80,64},{96,80},{112,96},{128,112},... | collective-permute-start | bytes 835592 | tf_op jit(solution)/shard_map/ppermute | solution.py:508
  86.4 8.4 %collective-permute-start.4 = (bf16[1088,128]{1,0:T(8,128)(2,1)S(1)}, bf16[1088,128]{1,0:T(8,128)(2,1)S(1)}, u32[]{:S(2)}, u32[]{:S(2)}) collective-permute-start(bf16[1088,128]{1,0:T(8,128)(2,1)S(1)} %shard_map.99.rest_3_), channel_id=1, source_target_pairs={{0,16},{16,32},{32,48},{48,64},{64,80},{80,96},{96,112},{112,128},... | collective-permute-start | bytes 835592 | tf_op jit(solution)/shard_map/ppermute | solution.py:508
  88.9 6.0 %collective-permute-start.3 = (bf16[1088,128]{1,0:T(8,128)(2,1)S(1)}, bf16[1088,128]{1,0:T(8,128)(2,1)S(1)}, u32[]{:S(2)}, u32[]{:S(2)}) collective-permute-start(bf16[1088,128]{1,0:T(8,128)(2,1)S(1)} %shard_map.101.rest_0_), channel_id=1, source_target_pairs={{16,0},{32,16},{48,32},{64,48},{80,64},{96,80},{112,96},{128,112},... | collective-permute-start | bytes 835592 | tf_op jit(solution)/shard_map/ppermute | solution.py:508
  89.5 5.4 %collective-permute-start.2 = (bf16[1088,128]{1,0:T(8,128)(2,1)S(1)}, bf16[1088,128]{1,0:T(8,128)(2,1)S(1)}, u32[]{:S(2)}, u32[]{:S(2)}) collective-permute-start(bf16[1088,128]{1,0:T(8,128)(2,1)S(1)} %shard_map.101.rest_0_), channel_id=1, source_target_pairs={{0,16},{16,32},{32,48},{48,64},{64,80},{80,96},{96,112},{112,128},... | collective-permute-start | bytes 835592 | tf_op jit(solution)/shard_map/ppermute | solution.py:508
  94.7 35.2 %copy-start.3 = (s32[1,256,32]{1,2,0:T(8,128)S(1)}, s32[1,256,32]{1,2,0:T(8,128)}, u32[]{:S(2)}) copy-start(s32[1,256,32]{1,2,0:T(8,128)} %param.11) | copy-start | bytes 98308

commit v4 on v3

--- a/solution.py
+++ b/solution.py
@@ -136,7 +136,7 @@
             acc_ref[c, pl.ds(at, 40), 0:72] += add[c * 40 : c * 40 + 40]
         return carry
 
-    lax.fori_loop(0, NZ // ZB, block, 0, unroll=16)
+    lax.fori_loop(0, NZ // ZB, block, 0, unroll=32)
 
 
 def fill_places(yv_ref, zv_ref):
@@ -283,7 +283,7 @@
             field[k, pl.ds(at, 64), :] = jnp.where(low, main, rim).astype(BF16)
         return carry
 
-    lax.fori_loop(0, N_PENCIL, take, 0, unroll=4)
+    lax.fori_loop(0, N_PENCIL, take, 0, unroll=16)
     along_z(field, col_ref, smooth, 2 * pair, 2)
     wide = lanes_of((128, 128)) < LANES
     for q in range(8):
@@ -396,7 +396,7 @@
             ot[pl.ds(r * LANES + 2 * b + 1, 1), :] = grads[r][:, 256:512]
         return carry
 
-    lax.fori_loop(0, NZ // ZB, block, 0, unroll=2)
+    lax.fori_loop(0, NZ // ZB, block, 0, unroll=16)
     for j in range(BACK):
         for h in range(2):
             piece = ot[j * 128 : j * 128 + 128, h * 128 : h * 128 + 128]

time: 132 us -> 128 us (0.970)
  Pallas kernels: 34.9 us -> 30.4 us
    pallas_call x1, Pallas kernels: 9.72 us -> 7.41 us  [per_device(): call(sample_kernel, shape((TILES * BACK, 128), BF16), [pltpu.VMEM((CH, NZ...]
  transfers between devices with their start and end apart: 7 -> 7, of which waited for: 3 -> 3; matrix products, arithmetic and copies ran while one was open for 9% -> 9% of each run, Pallas kernels for 7% -> 6%
where the time goes in v4:
time: 128 us; the launch traced here: 127 us
  blocking collectives  49.8 us (39%)
  Pallas kernels  30.4 us (24%)
  starting transfers between devices  24.7 us (19%)
  waiting for transfers between devices  10.4 us (8%)
  other arithmetic  9.78 us (8%)
  local copies, waits for them, and re-layouts  1.46 us (1%)
    all_to_all x1, blocking collectives, per_device(): lax.all_to_all(sampled.reshape(TILES, BACK, 128), both, split_axis=0, con...  25.3 us
    all_to_all x2, blocking collectives, per_device(): lax.all_to_all(lines, 'pencil', split_axis=0, concat_axis=0, tiled=True)  24.5 us
    all_to_all x1, starting transfers between devices, exchange(): rows = lax.all_to_all(rows, axes, split_axis=0, concat_axis=0, tiled=True)  15.7 us
    pallas_call x1, Pallas kernels, per_device(): call(sample_kernel, shape((TILES * BACK, 128), BF16), [pltpu.VMEM((CH, NZ...  7.41 us
    pallas_call x1, Pallas kernels, per_device(): pl.pallas_call(forward_kernel, out_shape=shape((N_PENCIL, CHUNK, 128), BF...  7.35 us
    all_to_all x1, waiting for transfers between devices, exchange(): rows = lax.all_to_all(rows, axes, split_axis=0, concat_axis=0, tiled=True)  7.16 us
    ppermute x2, starting transfers between devices, per_device(): lax.ppermute(field, 'slab', aft)  5.45 us
    convert_element_type x3, other arithmetic, correlation(): return (profile + jnp.where(distance == 0.0, 1.0, 0.0)).astype(BF16)  5.24 us
  transfers between devices with their start and end apart: 7, of which 3 were waited for; matrix products, arithmetic and copies ran while one was open for 9% of the time, Pallas kernels for 6%

profile of v4, /device:TPU:1, one launch (start us, length us, event | category | flops | bytes accessed | tf_op | source)
XLA Modules:
  0.0 127.3 jit_solution(3427329948142172941)
XLA Ops:
  0.6 2.8 %shard_map.95 = bf16[1536,128]{1,0:T(8,128)(2,1)} custom-call(f32[128,3,128]{2,1,0:T(4,128)} %bitcast.48, s32[128,3,128]{2,1,0:T(4,128)} %bitcast.49, bf16[128,4,128]{2,1,0:T(4,128)(2,1)} %bitcast.50, s32[32,256]{1,0:T(8,128)} %bitcast.44), custom_call_target="tpu_custom_call" | custom-call | tf_op jit(solution)/shard_map/pallas_call | solution.py:453
  3.4 15.7 %all-to-all-start = ((bf16[256,2,384]{2,1,0:T(2,128)(2,1)}), bf16[256,2,384]{2,1,0:T(2,128)(2,1)S(1)}, u32[]{:S(2)}, u32[]{:S(2)}) async-start(bf16[256,2,384]{2,1,0:T(2,128)(2,1)} %bitcast.46), calls=%async_computation | async-start | bytes 786432 | tf_op jit(solution)/shard_map/all_to_all | solution.py:426
  19.7 1.4 %fusion.32 = (f32[1]{0:T(128)}, f32[1]{0:T(128)}, f32[1]{0:T(128)}, f32[1]{0:T(128)}) fusion(f32[4]{0:T(128)} %param.12), kind=kLoop, calls=%fused_computation.63 | loop fusion | bytes 32 | tf_op jit(solution)/shard_map/gather | solution.py:448
  21.2 2.5 %multiply_multiply_fusion = (f32[128]{0:T(128)S(1)}, f32[128]{0:T(128)S(1)}) fusion(f32[]{:T(128)} %bitcast.17, f32[]{:T(128)} %bitcast.16, f32[]{:T(128)} %bitcast.15, f32[]{:T(128)} %bitcast.14), kind=kLoop, calls=%fused_computation.55 | loop fusion | flops 4096 | bytes 1040 | tf_op jit(solution)/shard_map/mul | solution.py:411
  24.2 0.9 negate_multiply_fusion
  25.5 2.7 %fusion.2 = (bf16[4,1024,256]{2,1,0:T(8,128)(2,1)S(1)}, bf16[4,1024,256]{2,1,0:T(8,128)(2,1)}) fusion(f32[1024,256]{1,0:T(8,128)S(1)} %get-tuple-element.27, f32[1024,256]{1,0:T(8,128)S(1)} %get-tuple-element.26, f32[4]{0:T(128)S(1)} %get-tuple-element.39, f32[4]{0:T(128)S(1)} %get-tuple-element.38, f32[1024,256]{1,0:T(8,128)S(1)} %get-tuple-element.31, ...), kind=kLoop, calls=%fused_computation.3 | loop fusion | flops 8388608 | bytes 8388640 | tf_op jit(solution)/shard_map/convert_element_type | solution.py:412
  28.2 2.2 %fusion.8.row_ref = bf16[4,256,1024]{2,1,0:T(8,128)(2,1)} fusion(f32[256,1024]{1,0:T(8,128)S(1)} %get-tuple-element.33, f32[4]{0:T(128)S(1)} %get-tuple-element.39, f32[4]{0:T(128)S(1)} %get-tuple-element.38, f32[256,1024]{1,0:T(8,128)S(1)} %get-tuple-element.32), kind=kLoop, calls=%fused_computation.11 | loop fusion | flops 4194304 | bytes 4194336 | tf_op jit(solution)/shard_map/convert_element_type | solution.py:412
  30.3 7.2 %all-to-all-done = bf16[256,2,384]{2,1,0:T(2,128)(2,1)S(1)} async-done(((bf16[256,2,384]{2,1,0:T(2,128)(2,1)}), bf16[256,2,384]{2,1,0:T(2,128)(2,1)S(1)}, u32[]{:S(2)}, u32[]{:S(2)}) %all-to-all-start) | async-done | bytes 393248 | tf_op jit(solution)/shard_map/all_to_all | solution.py:426
  37.5 1.7 %collective-permute-start = (bf16[1536,128]{1,0:T(8,128)(2,1)S(1)}, bf16[1536,128]{1,0:T(8,128)(2,1)S(1)}, u32[]{:S(2)}, u32[]{:S(2)}) collective-permute-start(bf16[1536,128]{1,0:T(8,128)(2,1)S(1)} %bitcast.38), channel_id=1, source_target_pairs={{0,16},{16,32},{32,48},{48,64},{64,80},{80,96},{96,112},{112,128},... | collective-permute-start | bytes 1179656 | tf_op jit(solution)/shard_map/ppermute | solution.py:463
  39.2 2.7 %shard_map.96 = (f32[4,1040,128]{2,1,0:T(8,128)S(1)}, f32[768,256]{1,0:T(8,128)S(1)}) custom-call(bf16[1536,128]{1,0:T(8,128)(2,1)S(1)} %bitcast.39), custom_call_target="tpu_custom_call" | custom-call | tf_op jit(solution)/shard_map/pallas_call | solution.py:468
  42.0 3.0 %collective-permute-done.1.dn_ref = bf16[1536,128]{1,0:T(8,128)(2,1)S(1)} collective-permute-done((bf16[1536,128]{1,0:T(8,128)(2,1)S(1)}, bf16[1536,128]{1,0:T(8,128)(2,1)S(1)}, u32[]{:S(2)}, u32[]{:S(2)}) %collective-permute-start.1) | collective-permute-done | bytes 393248 | tf_op jit(solution)/shard_map/ppermute | solution.py:464
  45.0 7.3 %shard_map.97 = bf16[16,136,128]{2,1,0:T(8,128)(2,1)S(1)} custom-call(bf16[1536,128]{1,0:T(8,128)(2,1)S(1)} %collective-permute-done.up_ref, bf16[1536,128]{1,0:T(8,128)(2,1)S(1)} %collective-permute-done.1.dn_ref, f32[4,1040,128]{2,1,0:T(8,128)S(1)} %get-tuple-element.14.start_ref, bf16[4,1024,256]{2,1,0:T(8,128)(2,1)} %get-tuple-element.15.col_ref), custom_call_target="tpu_custom_call" | custom-call | tf_op jit(solution)/shard_map/pallas_call | solution.py:475
  52.4 12.3 %all_to_all.20.in_ref = bf16[16,136,128]{2,1,0:T(8,128)(2,1)S(1)} all-to-all(bf16[16,136,128]{2,1,0:T(8,128)(2,1)S(1)} %shard_map.97), channel_id=1, replica_groups=mesh['slab'=16,'pencil'=16] {'pencil'}, dimensions={0} | all-to-all | bytes 1114112 | tf_op jit(solution)/shard_map/all_to_all | solution.py:489
  64.7 2.2 %shard_map.98 = (bf16[64,1024]{1,0:T(8,128)(2,1)}, bf16[16,136,128]{2,1,0:T(8,128)(2,1)S(1)}) custom-call(f32[4]{0:T(128)S(1)} %copy-done.4, bf16[16,136,128]{2,1,0:T(8,128)(2,1)S(1)} %all_to_all.20.in_ref, bf16[4,256,1024]{2,1,0:T(8,128)(2,1)S(1)} %copy-done, bf16[128,1024]{1,0:T(8,128)(2,1)S(1)} %fusion.24.rim_ref, f32[64,1024]{1,0:T(8,128)S(1)} %bitcast.42, ...), custom_call_target="tpu_custom_call" | custom-call | tf_op jit(solution)/shard_map/pallas_call | solution.py:490
  66.9 12.2 %all_to_all.21.in_ref = bf16[16,136,128]{2,1,0:T(8,128)(2,1)S(1)} all-to-all(bf16[16,136,128]{2,1,0:T(8,128)(2,1)S(1)} %get-tuple-element.18), channel_id=1, replica_groups=mesh['slab'=16,'pencil'=16] {'pencil'}, dimensions={0} | all-to-all | bytes 1114112 | tf_op jit(solution)/shard_map/all_to_all | solution.py:497
  79.1 1.3 %shard_map.99.rest_3_ = bf16[1088,128]{1,0:T(8,128)(2,1)S(1)} custom-call(bf16[16,136,128]{2,1,0:T(8,128)(2,1)S(1)} %all_to_all.21.in_ref, bf16[4,1024,256]{2,1,0:T(8,128)(2,1)S(1)} %get-tuple-element.19.col_ref), custom_call_target="tpu_custom_call" | custom-call | tf_op jit(solution)/shard_map/pallas_call | solution.py:500
  80.4 4.9 %collective-permute-start.5 = (bf16[1088,128]{1,0:T(8,128)(2,1)S(1)}, bf16[1088,128]{1,0:T(8,128)(2,1)S(1)}, u32[]{:S(2)}, u32[]{:S(2)}) collective-permute-start(bf16[1088,128]{1,0:T(8,128)(2,1)S(1)} %shard_map.99.rest_3_), channel_id=1, source_target_pairs={{16,0},{32,16},{48,32},{64,48},{80,64},{96,80},{112,96},{128,112},... | collective-permute-start | bytes 835592 | tf_op jit(solution)/shard_map/ppermute | solution.py:508
  85.3 0.7 collective-permute-start.4
  85.9 1.3 %shard_map.101.rest_0_ = bf16[1088,128]{1,0:T(8,128)(2,1)S(1)} custom-call(bf16[16,136,128]{2,1,0:T(8,128)(2,1)S(1)} %all_to_all.21.in_ref, bf16[4,1024,256]{2,1,0:T(8,128)(2,1)S(1)} %get-tuple-element.19.col_ref), custom_call_target="tpu_custom_call" | custom-call | tf_op jit(solution)/shard_map/pallas_call | solution.py:500
  87.8 1.2 collective-permute-start.2
  89.0 4.1 %shard_map.100.planes = bf16[32,208,1536]{2,1,0:T(8,128)(2,1)S(1)} custom-call(f32[768,256]{1,0:T(8,128)S(1)} %get-tuple-element.21.xt_ref), custom_call_target="tpu_custom_call" | custom-call | flops 60000000 | bytes 21000000 | tf_op jit(solution)/shard_map/pallas_call | solution.py:509
  93.3 7.4 %shard_map.102 = bf16[1024,128]{1,0:T(8,128)(2,1)S(1)} custom-call(bf16[32,208,1536]{2,1,0:T(8,128)(2,1)S(1)} %shard_map.100.planes, f32[768,256]{1,0:T(8,128)S(1)} %get-tuple-element.21.xt_ref, bf16[1088,128]{1,0:T(8,128)(2,1)S(1)} %shard_map.101.rest_0_, bf16[1088,128]{1,0:T(8,128)(2,1)S(1)} %collective-permute-done.2.rest_1_, ...), custom_call_target="tpu_custom_call" | custom-call | tf_op jit(solution)/shard_map/pallas_call | solution.py:516
  100.7 25.3 %all_to_all.22 = bf16[256,4,128]{2,1,0:T(4,128)(2,1)S(1)} all-to-all(bf16[256,4,128]{2,1,0:T(4,128)(2,1)S(1)} %bitcast.40), channel_id=1, replica_groups=mesh['slab'=16,'pencil'=16] {'slab','pencil'}, dimensions={0} | all-to-all | bytes 524288 | tf_op jit(solution)/shard_map/all_to_all | solution.py:526
  126.0 1.3 %shard_map.103 = f32[128,7,128]{2,1,0:T(8,128)} custom-call(bf16[1024,128]{1,0:T(8,128)(2,1)S(1)} %bitcast.41, s32[32,256]{1,0:T(8,128)S(1)} %bitcast.45), custom_call_target="tpu_custom_call" | custom-call | tf_op jit(solution)/shard_map/pallas_call | solution.py:529
  (25 shorter events, 2.4 us)
Async XLA Ops:
  3.4 34.1 %all-to-all-start = ((bf16[256,2,384]{2,1,0:T(2,128)(2,1)}), bf16[256,2,384]{2,1,0:T(2,128)(2,1)S(1)}, u32[]{:S(2)}, u32[]{:S(2)}) async-start(bf16[256,2,384]{2,1,0:T(2,128)(2,1)} %bitcast.46), calls=%async_computation | async-start | bytes 786432 | tf_op jit(solution)/shard_map/all_to_all | solution.py:426
  30.3 34.3 %copy-start.1 = (f32[1,64,1024]{2,1,0:T(8,128)S(1)}, f32[1,64,1024]{2,1,0:T(8,128)}, u32[]{:S(2)}) copy-start(f32[1,64,1024]{2,1,0:T(8,128)} %param.14) | copy-start | bytes 786436
  30.3 34.3 %copy-start.2 = (f32[1,64,1024]{2,1,0:T(8,128)S(1)}, f32[1,64,1024]{2,1,0:T(8,128)}, u32[]{:S(2)}) copy-start(f32[1,64,1024]{2,1,0:T(8,128)} %param.15) | copy-start | bytes 786436
  30.3 34.3 %copy-start.4 = (f32[4]{0:T(128)S(1)}, f32[4]{0:T(128)}, u32[]{:S(2)}) copy-start(f32[4]{0:T(128)} %bias_ref.1) | copy-start | bytes 52
  37.5 27.2 %copy-start = (bf16[4,256,1024]{2,1,0:T(8,128)(2,1)S(1)}, bf16[4,256,1024]{2,1,0:T(8,128)(2,1)}, u32[]{:S(2)}) copy-start(bf16[4,256,1024]{2,1,0:T(8,128)(2,1)} %fusion.8.row_ref) | copy-start | bytes 6291460
  37.5 7.5 %collective-permute-start.1 = (bf16[1536,128]{1,0:T(8,128)(2,1)S(1)}, bf16[1536,128]{1,0:T(8,128)(2,1)S(1)}, u32[]{:S(2)}, u32[]{:S(2)}) collective-permute-start(bf16[1536,128]{1,0:T(8,128)(2,1)S(1)} %bitcast.37), channel_id=1, source_target_pairs={{16,0},{32,16},{48,32},{64,48},{80,64},{96,80},{112,96},{128,112},... | collective-permute-start | bytes 1179656 | tf_op jit(solution)/shard_map/ppermute | solution.py:464
  37.5 7.5 %collective-permute-start = (bf16[1536,128]{1,0:T(8,128)(2,1)S(1)}, bf16[1536,128]{1,0:T(8,128)(2,1)S(1)}, u32[]{:S(2)}, u32[]{:S(2)}) collective-permute-start(bf16[1536,128]{1,0:T(8,128)(2,1)S(1)} %bitcast.38), channel_id=1, source_target_pairs={{0,16},{16,32},{32,48},{48,64},{64,80},{80,96},{96,112},{112,128},... | collective-permute-start | bytes 1179656 | tf_op jit(solution)/shard_map/ppermute | solution.py:463
  80.4 12.7 %collective-permute-start.5 = (bf16[1088,128]{1,0:T(8,128)(2,1)S(1)}, bf16[1088,128]{1,0:T(8,128)(2,1)S(1)}, u32[]{:S(2)}, u32[]{:S(2)}) collective-permute-start(bf16[1088,128]{1,0:T(8,128)(2,1)S(1)} %shard_map.99.rest_3_), channel_id=1, source_target_pairs={{16,0},{32,16},{48,32},{64,48},{80,64},{96,80},{112,96},{128,112},... | collective-permute-start | bytes 835592 | tf_op jit(solution)/shard_map/ppermute | solution.py:508
  85.3 7.8 %collective-permute-start.4 = (bf16[1088,128]{1,0:T(8,128)(2,1)S(1)}, bf16[1088,128]{1,0:T(8,128)(2,1)S(1)}, u32[]{:S(2)}, u32[]{:S(2)}) collective-permute-start(bf16[1088,128]{1,0:T(8,128)(2,1)S(1)} %shard_map.99.rest_3_), channel_id=1, source_target_pairs={{0,16},{16,32},{32,48},{48,64},{64,80},{80,96},{96,112},{112,128},... | collective-permute-start | bytes 835592 | tf_op jit(solution)/shard_map/ppermute | solution.py:508
  87.2 6.1 %collective-permute-start.3 = (bf16[1088,128]{1,0:T(8,128)(2,1)S(1)}, bf16[1088,128]{1,0:T(8,128)(2,1)S(1)}, u32[]{:S(2)}, u32[]{:S(2)}) collective-permute-start(bf16[1088,128]{1,0:T(8,128)(2,1)S(1)} %shard_map.101.rest_0_), channel_id=1, source_target_pairs={{16,0},{32,16},{48,32},{64,48},{80,64},{96,80},{112,96},{128,112},... | collective-permute-start | bytes 835592 | tf_op jit(solution)/shard_map/ppermute | solution.py:508
  87.8 5.5 %collective-permute-start.2 = (bf16[1088,128]{1,0:T(8,128)(2,1)S(1)}, bf16[1088,128]{1,0:T(8,128)(2,1)S(1)}, u32[]{:S(2)}, u32[]{:S(2)}) collective-permute-start(bf16[1088,128]{1,0:T(8,128)(2,1)S(1)} %shard_map.101.rest_0_), channel_id=1, source_target_pairs={{0,16},{16,32},{32,48},{48,64},{64,80},{80,96},{96,112},{112,128},... | collective-permute-start | bytes 835592 | tf_op jit(solution)/shard_map/ppermute | solution.py:508
  93.1 32.9 %copy-start.3 = (s32[1,256,32]{1,2,0:T(8,128)S(1)}, s32[1,256,32]{1,2,0:T(8,128)}, u32[]{:S(2)}) copy-start(s32[1,256,32]{1,2,0:T(8,128)} %param.11) | copy-start | bytes 98308

commit v5 on v4

--- a/solution.py
+++ b/solution.py
@@ -1,5 +1,3 @@
-import functools
-
 import jax
 import jax.numpy as jnp
 from jax import lax
@@ -27,6 +25,7 @@
 
 
 PAIRS = RECORD // 128
+PART = NZ + 64
 BACK = 4
 
 
@@ -268,7 +267,7 @@
         out_ref[p, 128:136, :] = rims[p * 8 : p * 8 + 8]
 
 
-def adjoint_kernel(pair, in_ref, col_ref, out_ref, field, smooth):
+def adjoint_kernel(in_ref, col_ref, out_ref, field, smooth):
     lane = lanes_of((64, 128))
     low = lane < LANES
 
@@ -276,21 +275,25 @@
         at = pl.multiple_of(p * 64, 64)
         rims = in_ref[p, 128:136, :].astype(F32)
         table = jnp.concatenate([rims, jnp.zeros((120, 128), F32)], axis=0).T[0:64]
-        both = in_ref[p, pair * 64 : pair * 64 + 64, :].astype(F32)
-        for k in range(2):
-            main = both if k == 0 else pltpu.roll(both, LANES, 1)
-            rim = jnp.where(lane < 66, pltpu.roll(table, LANES - 2 * (2 * pair + k), 1), 0.0)
-            field[k, pl.ds(at, 64), :] = jnp.where(low, main, rim).astype(BF16)
+        for pair in range(2):
+            both = in_ref[p, pair * 64 : pair * 64 + 64, :].astype(F32)
+            for k in range(2):
+                c = 2 * pair + k
+                main = both if k == 0 else pltpu.roll(both, LANES, 1)
+                rim = jnp.where(lane < 66, pltpu.roll(table, LANES - 2 * c, 1), 0.0)
+                field[c, pl.ds(at, 64), :] = jnp.where(low, main, rim).astype(BF16)
         return carry
 
     lax.fori_loop(0, N_PENCIL, take, 0, unroll=16)
-    along_z(field, col_ref, smooth, 2 * pair, 2)
+    along_z(field, col_ref, smooth, 0, CH)
     wide = lanes_of((128, 128)) < LANES
-    for q in range(8):
-        parts = [smooth[k, q * 128 : q * 128 + 128, :] for k in range(2)]
-        both = jnp.where(wide, parts[0], pltpu.roll(parts[1], LANES, 1))
-        out_ref[q * 128 : q * 128 + 128, :] = both.astype(BF16)
-        out_ref[NZ + q * 8 : NZ + q * 8 + 8, :] = rim_rows(parts, 128).astype(BF16)
+    for pair in range(2):
+        base = pair * PART
+        for q in range(8):
+            parts = [smooth[2 * pair + k, q * 128 : q * 128 + 128, :] for k in range(2)]
+            both = jnp.where(wide, parts[0], pltpu.roll(parts[1], LANES, 1))
+            out_ref[base + q * 128 : base + q * 128 + 128, :] = both.astype(BF16)
+            out_ref[base + NZ + q * 8 : base + NZ + q * 8 + 8, :] = rim_rows(parts, 128).astype(BF16)
 
 
 def write_planes(xt_ref, b, places, planes):
@@ -334,13 +337,13 @@
 
     def fill(q, carry):
         at = pl.multiple_of(q * 128, 128)
-        rim_at = pl.multiple_of(NZ + q * 8, 8)
         for pair in range(2):
+            rim_at = pl.multiple_of(pair * PART + NZ + q * 8, 8)
             tables = []
-            for ref in refs[pair]:
+            for ref in refs:
                 rims = ref[pl.ds(rim_at, 8), :].astype(F32)
                 tables.append(jnp.concatenate([rims, jnp.zeros((120, 128), F32)], axis=0).T)
-            own, up, dn = (ref[pl.ds(at, 128), :].astype(F32) for ref in refs[pair])
+            own, up, dn = (ref[pl.ds(pair * PART + at, 128), :].astype(F32) for ref in refs)
             for k in range(2):
                 c = 2 * pair + k
                 if k == 0:
@@ -362,7 +365,7 @@
 
 
 def sample_kernel(planes, xt_ref, *rest):
-    refs, (out_ref, field, ot, tall) = (rest[0:3], rest[3:6]), rest[6:]
+    refs, (out_ref, field, ot, tall) = rest[0:3], rest[3:]
     fill_field(refs, field)
     zv = lax.broadcasted_iota(jnp.int32, (40, 512), 0).astype(F32)
     ot[GRADS:, :] = jnp.zeros((LANES, TILES), F32)
@@ -495,17 +498,14 @@
         compiler_params=params(20),
     )(bias_values, lines, k_row, k_rim, observed[0], precision[0])
     lines = lax.all_to_all(lines, "pencil", split_axis=0, concat_axis=0, tiled=True)
-    fields = []
-    for pair in range(2):
-        field = call(
-            functools.partial(adjoint_kernel, pair),
-            shape((NZ + 64, 128), BF16),
-            [pltpu.VMEM((2, NZ, 128), BF16), pltpu.VMEM((2, NZ, 128), F32)],
-            16,
-        )(lines, k_back)
-        if pair == 1:
-            field, late = lax.optimization_barrier((field, xt))
-        fields += [field, lax.ppermute(field, "slab", forth), lax.ppermute(field, "slab", aft)]
+    field = call(
+        adjoint_kernel,
+        shape((2 * PART, 128), BF16),
+        [pltpu.VMEM((CH, NZ, 128), BF16), pltpu.VMEM((CH, NZ, 128), F32)],
+        16,
+    )(lines, k_back)
+    field, late = lax.optimization_barrier((field, xt))
+    fields = [field, lax.ppermute(field, "slab", forth), lax.ppermute(field, "slab", aft)]
     planes = pl.pallas_call(
         weights_kernel,
         out_shape=shape((NZ // ZB, 208, 1536), BF16),

time: 128 us -> 128 us (level)
  waiting for transfers between devices: 10.4 us -> 13.4 us
  starting transfers between devices: 24.7 us -> 22.9 us
  blocking collectives: 49.8 us -> 48.5 us
    ppermute x2 -> x1, waiting for transfers between devices: 0.19 us -> 3.41 us  [per_device(): lax.ppermute(field, 'slab', aft)]
    ppermute x2 -> x1, starting transfers between devices: 1.83 us -> 0.48 us  [per_device(): lax.ppermute(field, 'slab', forth)]
    ppermute x2 -> x1, starting transfers between devices: 5.45 us -> 5.05 us  [per_device(): lax.ppermute(field, 'slab', aft)]
    pallas_call x2 -> x1, Pallas kernels: 2.58 us -> 2.77 us  [per_device(): call(adjoint_kernel, shape((2 * PART, 128), BF16), [pltpu.VMEM((CH, NZ, 1...]
  transfers between devices with their start and end apart: 7 -> 5, of which waited for: 3 -> 3; matrix products, arithmetic and copies ran while one was open for 9% -> 9% of each run, Pallas kernels for 6% -> 5%
where the time goes in v5:
time: 128 us
  blocking collectives  48.5 us (38%)
  Pallas kernels  30.6 us (24%)
  starting transfers between devices  22.9 us (18%)
  waiting for transfers between devices  13.4 us (10%)
  other arithmetic  9.92 us (8%)
  local copies, waits for them, and re-layouts  1.51 us (1%)
    all_to_all x2, blocking collectives, per_device(): lax.all_to_all(lines, 'pencil', split_axis=0, concat_axis=0, tiled=True)  24.5 us
    all_to_all x1, blocking collectives, per_device(): lax.all_to_all(sampled.reshape(TILES, BACK, 128), both, split_axis=0, con...  24 us
    all_to_all x1, starting transfers between devices, exchange(): rows = lax.all_to_all(rows, axes, split_axis=0, concat_axis=0, tiled=True)  15.7 us
    pallas_call x1, Pallas kernels, per_device(): call(sample_kernel, shape((TILES * BACK, 128), BF16), [pltpu.VMEM((CH, NZ...  7.42 us
    pallas_call x1, Pallas kernels, per_device(): pl.pallas_call(forward_kernel, out_shape=shape((N_PENCIL, CHUNK, 128), BF...  7.35 us
    all_to_all x1, waiting for transfers between devices, exchange(): rows = lax.all_to_all(rows, axes, split_axis=0, concat_axis=0, tiled=True)  6.97 us
    convert_element_type x3, other arithmetic, correlation(): return (profile + jnp.where(distance == 0.0, 1.0, 0.0)).astype(BF16)  5.26 us
    ppermute x1, starting transfers between devices, per_device(): lax.ppermute(field, 'slab', aft)  5.05 us
  transfers between devices with their start and end apart: 5, of which 3 were waited for; matrix products, arithmetic and copies ran while one was open for 9% of the time, Pallas kernels for 5%

profile of v5, /device:TPU:1, one launch (start us, length us, event | category | flops | bytes accessed | tf_op | source)
XLA Modules:
  0.0 127.7 jit_solution(13251741110568053102)
XLA Ops:
  0.6 2.8 %shard_map.95 = bf16[1536,128]{1,0:T(8,128)(2,1)} custom-call(f32[128,3,128]{2,1,0:T(4,128)} %bitcast.48, s32[128,3,128]{2,1,0:T(4,128)} %bitcast.49, bf16[128,4,128]{2,1,0:T(4,128)(2,1)} %bitcast.50, s32[32,256]{1,0:T(8,128)} %bitcast.44), custom_call_target="tpu_custom_call" | custom-call | tf_op jit(solution)/shard_map/pallas_call | solution.py:456
  3.4 15.7 %all-to-all-start = ((bf16[256,2,384]{2,1,0:T(2,128)(2,1)}), bf16[256,2,384]{2,1,0:T(2,128)(2,1)S(1)}, u32[]{:S(2)}, u32[]{:S(2)}) async-start(bf16[256,2,384]{2,1,0:T(2,128)(2,1)} %bitcast.46), calls=%async_computation | async-start | bytes 786432 | tf_op jit(solution)/shard_map/all_to_all | solution.py:429
  19.1 0.7 multiply_multiply_fusion.1
  19.7 1.5 %fusion.32 = (f32[1]{0:T(128)}, f32[1]{0:T(128)}, f32[1]{0:T(128)}, f32[1]{0:T(128)}) fusion(f32[4]{0:T(128)} %param.12), kind=kLoop, calls=%fused_computation.63 | loop fusion | bytes 32 | tf_op jit(solution)/shard_map/gather | solution.py:451
  21.2 2.6 %multiply_multiply_fusion = (f32[128]{0:T(128)S(1)}, f32[128]{0:T(128)S(1)}) fusion(f32[]{:T(128)} %bitcast.17, f32[]{:T(128)} %bitcast.16, f32[]{:T(128)} %bitcast.15, f32[]{:T(128)} %bitcast.14), kind=kLoop, calls=%fused_computation.55 | loop fusion | flops 4096 | bytes 1040 | tf_op jit(solution)/shard_map/mul | solution.py:414
  24.3 0.9 negate_multiply_fusion
  25.7 2.7 %fusion.2 = (bf16[4,1024,256]{2,1,0:T(8,128)(2,1)S(1)}, bf16[4,1024,256]{2,1,0:T(8,128)(2,1)}) fusion(f32[1024,256]{1,0:T(8,128)S(1)} %get-tuple-element.27, f32[1024,256]{1,0:T(8,128)S(1)} %get-tuple-element.26, f32[4]{0:T(128)S(1)} %get-tuple-element.39, f32[4]{0:T(128)S(1)} %get-tuple-element.38, f32[1024,256]{1,0:T(8,128)S(1)} %get-tuple-element.31, ...), kind=kLoop, calls=%fused_computation.3 | loop fusion | flops 8388608 | bytes 8388640 | tf_op jit(solution)/shard_map/convert_element_type | solution.py:415
  28.3 2.2 %fusion.8.row_ref = bf16[4,256,1024]{2,1,0:T(8,128)(2,1)} fusion(f32[256,1024]{1,0:T(8,128)S(1)} %get-tuple-element.33, f32[4]{0:T(128)S(1)} %get-tuple-element.39, f32[4]{0:T(128)S(1)} %get-tuple-element.38, f32[256,1024]{1,0:T(8,128)S(1)} %get-tuple-element.32), kind=kLoop, calls=%fused_computation.11 | loop fusion | flops 4194304 | bytes 4194336 | tf_op jit(solution)/shard_map/convert_element_type | solution.py:415
  30.5 7.0 %all-to-all-done = bf16[256,2,384]{2,1,0:T(2,128)(2,1)S(1)} async-done(((bf16[256,2,384]{2,1,0:T(2,128)(2,1)}), bf16[256,2,384]{2,1,0:T(2,128)(2,1)S(1)}, u32[]{:S(2)}, u32[]{:S(2)}) %all-to-all-start) | async-done | bytes 393248 | tf_op jit(solution)/shard_map/all_to_all | solution.py:429
  37.5 1.7 %collective-permute-start = (bf16[1536,128]{1,0:T(8,128)(2,1)S(1)}, bf16[1536,128]{1,0:T(8,128)(2,1)S(1)}, u32[]{:S(2)}, u32[]{:S(2)}) collective-permute-start(bf16[1536,128]{1,0:T(8,128)(2,1)S(1)} %bitcast.38), channel_id=1, source_target_pairs={{0,16},{16,32},{32,48},{48,64},{64,80},{80,96},{96,112},{112,128},... | collective-permute-start | bytes 1179656 | tf_op jit(solution)/shard_map/ppermute | solution.py:466
  39.2 2.7 %shard_map.96 = (f32[4,1040,128]{2,1,0:T(8,128)S(1)}, f32[768,256]{1,0:T(8,128)S(1)}) custom-call(bf16[1536,128]{1,0:T(8,128)(2,1)S(1)} %bitcast.39), custom_call_target="tpu_custom_call" | custom-call | tf_op jit(solution)/shard_map/pallas_call | solution.py:471
  42.0 3.0 %collective-permute-done.1.dn_ref = bf16[1536,128]{1,0:T(8,128)(2,1)S(1)} collective-permute-done((bf16[1536,128]{1,0:T(8,128)(2,1)S(1)}, bf16[1536,128]{1,0:T(8,128)(2,1)S(1)}, u32[]{:S(2)}, u32[]{:S(2)}) %collective-permute-start.1) | collective-permute-done | bytes 393248 | tf_op jit(solution)/shard_map/ppermute | solution.py:467
  45.0 7.3 %shard_map.97 = bf16[16,136,128]{2,1,0:T(8,128)(2,1)S(1)} custom-call(bf16[1536,128]{1,0:T(8,128)(2,1)S(1)} %collective-permute-done.up_ref, bf16[1536,128]{1,0:T(8,128)(2,1)S(1)} %collective-permute-done.1.dn_ref, f32[4,1040,128]{2,1,0:T(8,128)S(1)} %get-tuple-element.14.start_ref, bf16[4,1024,256]{2,1,0:T(8,128)(2,1)} %get-tuple-element.15.col_ref), custom_call_target="tpu_custom_call" | custom-call | tf_op jit(solution)/shard_map/pallas_call | solution.py:478
  52.4 12.4 %all_to_all.20.in_ref = bf16[16,136,128]{2,1,0:T(8,128)(2,1)S(1)} all-to-all(bf16[16,136,128]{2,1,0:T(8,128)(2,1)S(1)} %shard_map.97), channel_id=1, replica_groups=mesh['slab'=16,'pencil'=16] {'pencil'}, dimensions={0} | all-to-all | bytes 1114112 | tf_op jit(solution)/shard_map/all_to_all | solution.py:492
  64.7 2.2 %shard_map.98 = (bf16[64,1024]{1,0:T(8,128)(2,1)}, bf16[16,136,128]{2,1,0:T(8,128)(2,1)S(1)}) custom-call(f32[4]{0:T(128)S(1)} %copy-done.4, bf16[16,136,128]{2,1,0:T(8,128)(2,1)S(1)} %all_to_all.20.in_ref, bf16[4,256,1024]{2,1,0:T(8,128)(2,1)S(1)} %copy-done, bf16[128,1024]{1,0:T(8,128)(2,1)S(1)} %fusion.24.rim_ref, f32[64,1024]{1,0:T(8,128)S(1)} %bitcast.42, ...), custom_call_target="tpu_custom_call" | custom-call | tf_op jit(solution)/shard_map/pallas_call | solution.py:493
  66.9 12.2 %all_to_all.21.in_ref = bf16[16,136,128]{2,1,0:T(8,128)(2,1)S(1)} all-to-all(bf16[16,136,128]{2,1,0:T(8,128)(2,1)S(1)} %get-tuple-element.18), channel_id=1, replica_groups=mesh['slab'=16,'pencil'=16] {'pencil'}, dimensions={0} | all-to-all | bytes 1114112 | tf_op jit(solution)/shard_map/all_to_all | solution.py:500
  79.1 2.8 %shard_map.99.rest_0_ = bf16[2176,128]{1,0:T(8,128)(2,1)S(1)} custom-call(bf16[16,136,128]{2,1,0:T(8,128)(2,1)S(1)} %all_to_all.21.in_ref, bf16[4,1024,256]{2,1,0:T(8,128)(2,1)S(1)} %get-tuple-element.19.col_ref), custom_call_target="tpu_custom_call" | custom-call | tf_op jit(solution)/shard_map/pallas_call | solution.py:501
  81.9 5.0 %collective-permute-start.3 = (bf16[2176,128]{1,0:T(8,128)(2,1)S(1)}, bf16[2176,128]{1,0:T(8,128)(2,1)S(1)}, u32[]{:S(2)}, u32[]{:S(2)}) collective-permute-start(bf16[2176,128]{1,0:T(8,128)(2,1)S(1)} %shard_map.99.rest_0_), channel_id=1, source_target_pairs={{16,0},{32,16},{48,32},{64,48},{80,64},{96,80},{112,96},{128,112},... | collective-permute-start | bytes 1671176 | tf_op jit(solution)/shard_map/ppermute | solution.py:508
  86.9 0.5 collective-permute-start.2
  87.4 4.1 %shard_map.100.planes = bf16[32,208,1536]{2,1,0:T(8,128)(2,1)S(1)} custom-call(f32[768,256]{1,0:T(8,128)S(1)} %get-tuple-element.21.xt_ref), custom_call_target="tpu_custom_call" | custom-call | flops 60000000 | bytes 21000000 | tf_op jit(solution)/shard_map/pallas_call | solution.py:509
  91.5 3.4 %collective-permute-done.3.rest_2_ = bf16[2176,128]{1,0:T(8,128)(2,1)S(1)} collective-permute-done((bf16[2176,128]{1,0:T(8,128)(2,1)S(1)}, bf16[2176,128]{1,0:T(8,128)(2,1)S(1)}, u32[]{:S(2)}, u32[]{:S(2)}) %collective-permute-start.3) | collective-permute-done | bytes 557088 | tf_op jit(solution)/shard_map/ppermute | solution.py:508
  94.9 7.4 %shard_map.101 = bf16[1024,128]{1,0:T(8,128)(2,1)S(1)} custom-call(bf16[32,208,1536]{2,1,0:T(8,128)(2,1)S(1)} %shard_map.100.planes, f32[768,256]{1,0:T(8,128)S(1)} %get-tuple-element.21.xt_ref, bf16[2176,128]{1,0:T(8,128)(2,1)S(1)} %shard_map.99.rest_0_, bf16[2176,128]{1,0:T(8,128)(2,1)S(1)} %collective-permute-done.2.rest_1_, ...), custom_call_target="tpu_custom_call" | custom-call | tf_op jit(solution)/shard_map/pallas_call | solution.py:516
  102.3 24.0 %all_to_all.22 = bf16[256,4,128]{2,1,0:T(4,128)(2,1)S(1)} all-to-all(bf16[256,4,128]{2,1,0:T(4,128)(2,1)S(1)} %bitcast.40), channel_id=1, replica_groups=mesh['slab'=16,'pencil'=16] {'slab','pencil'}, dimensions={0} | all-to-all | bytes 524288 | tf_op jit(solution)/shard_map/all_to_all | solution.py:526
  126.4 1.3 %shard_map.102 = f32[128,7,128]{2,1,0:T(8,128)} custom-call(bf16[1024,128]{1,0:T(8,128)(2,1)S(1)} %bitcast.41, s32[32,256]{1,0:T(8,128)S(1)} %bitcast.45), custom_call_target="tpu_custom_call" | custom-call | tf_op jit(solution)/shard_map/pallas_call | solution.py:529
  (20 shorter events, 0.9 us)
Async XLA Ops:
  3.4 34.1 %all-to-all-start = ((bf16[256,2,384]{2,1,0:T(2,128)(2,1)}), bf16[256,2,384]{2,1,0:T(2,128)(2,1)S(1)}, u32[]{:S(2)}, u32[]{:S(2)}) async-start(bf16[256,2,384]{2,1,0:T(2,128)(2,1)} %bitcast.46), calls=%async_computation | async-start | bytes 786432 | tf_op jit(solution)/shard_map/all_to_all | solution.py:429
  30.5 34.2 %copy-start.1 = (f32[1,64,1024]{2,1,0:T(8,128)S(1)}, f32[1,64,1024]{2,1,0:T(8,128)}, u32[]{:S(2)}) copy-start(f32[1,64,1024]{2,1,0:T(8,128)} %param.14) | copy-start | bytes 786436
  30.5 34.2 %copy-start.2 = (f32[1,64,1024]{2,1,0:T(8,128)S(1)}, f32[1,64,1024]{2,1,0:T(8,128)}, u32[]{:S(2)}) copy-start(f32[1,64,1024]{2,1,0:T(8,128)} %param.15) | copy-start | bytes 786436
  30.5 34.2 %copy-start.4 = (f32[4]{0:T(128)S(1)}, f32[4]{0:T(128)}, u32[]{:S(2)}) copy-start(f32[4]{0:T(128)} %bias_ref.1) | copy-start | bytes 52
  37.5 27.2 %copy-start = (bf16[4,256,1024]{2,1,0:T(8,128)(2,1)S(1)}, bf16[4,256,1024]{2,1,0:T(8,128)(2,1)}, u32[]{:S(2)}) copy-start(bf16[4,256,1024]{2,1,0:T(8,128)(2,1)} %fusion.8.row_ref) | copy-start | bytes 6291460
  37.5 7.5 %collective-permute-start.1 = (bf16[1536,128]{1,0:T(8,128)(2,1)S(1)}, bf16[1536,128]{1,0:T(8,128)(2,1)S(1)}, u32[]{:S(2)}, u32[]{:S(2)}) collective-permute-start(bf16[1536,128]{1,0:T(8,128)(2,1)S(1)} %bitcast.37), channel_id=1, source_target_pairs={{16,0},{32,16},{48,32},{64,48},{80,64},{96,80},{112,96},{128,112},... | collective-permute-start | bytes 1179656 | tf_op jit(solution)/shard_map/ppermute | solution.py:467
  37.5 7.5 %collective-permute-start = (bf16[1536,128]{1,0:T(8,128)(2,1)S(1)}, bf16[1536,128]{1,0:T(8,128)(2,1)S(1)}, u32[]{:S(2)}, u32[]{:S(2)}) collective-permute-start(bf16[1536,128]{1,0:T(8,128)(2,1)S(1)} %bitcast.38), channel_id=1, source_target_pairs={{0,16},{16,32},{32,48},{48,64},{64,80},{80,96},{96,112},{112,128},... | collective-permute-start | bytes 1179656 | tf_op jit(solution)/shard_map/ppermute | solution.py:466
  81.9 13.0 %collective-permute-start.3 = (bf16[2176,128]{1,0:T(8,128)(2,1)S(1)}, bf16[2176,128]{1,0:T(8,128)(2,1)S(1)}, u32[]{:S(2)}, u32[]{:S(2)}) collective-permute-start(bf16[2176,128]{1,0:T(8,128)(2,1)S(1)} %shard_map.99.rest_0_), channel_id=1, source_target_pairs={{16,0},{32,16},{48,32},{64,48},{80,64},{96,80},{112,96},{128,112},... | collective-permute-start | bytes 1671176 | tf_op jit(solution)/shard_map/ppermute | solution.py:508
  86.9 8.0 %collective-permute-start.2 = (bf16[2176,128]{1,0:T(8,128)(2,1)S(1)}, bf16[2176,128]{1,0:T(8,128)(2,1)S(1)}, u32[]{:S(2)}, u32[]{:S(2)}) collective-permute-start(bf16[2176,128]{1,0:T(8,128)(2,1)S(1)} %shard_map.99.rest_0_), channel_id=1, source_target_pairs={{0,16},{16,32},{32,48},{48,64},{64,80},{80,96},{96,112},{112,128},... | collective-permute-start | bytes 1671176 | tf_op jit(solution)/shard_map/ppermute | solution.py:508
  91.5 34.9 %copy-start.3 = (s32[1,256,32]{1,2,0:T(8,128)S(1)}, s32[1,256,32]{1,2,0:T(8,128)}, u32[]{:S(2)}) copy-start(s32[1,256,32]{1,2,0:T(8,128)} %param.11) | copy-start | bytes 98308
